TPU v7x, 256 devices: a whole 4x4x8 slice. The times are simulated.
256 devices in a mesh: tile: 256 (over z, y, x, core).
Axes of the slice: x: 4, y: 4, z: 8, core: 2. Of those that a mesh axis runs over, the one named last changes fastest.
Arguments:
- adjoint_zonal: bfloat16 [32, 8, 4096, 128], P(None, None, 'tile'), may hold values from -70 to 70
- adjoint_meridional: bfloat16 [32, 8, 4096, 128], P(None, None, 'tile'), may hold values from -70 to 70
- cell_fraction: bfloat16 [8, 4096, 128], P(None, 'tile'), may hold values from 0.19921875 to 1
- level_thickness: float32 [8], replicated, may hold values from 0.5 to 2
- land_mask: int32 [4096, 128], P('tile'), may hold values 0 or 1
- edge_codes: int32 [256, 4], P('tile'), may hold values from 0 to 1, as said below
Outputs:
- surface_adjoint: float32 [32, 4096, 128], P(None, 'tile')
- residual: float32 [32, 4096, 128], P(None, 'tile')
Inputs may be any that keep to these rules, and one draw needn't show every extreme that they name: edge_codes[t, 1] equals edge_codes[t - 1, 0] and edge_codes[t, 3] equals edge_codes[t - 16, 2], tile numbers taken modulo 256.
All inputs are finite; a program needn't handle non-finite values. No bound on the sum of `land_mask` on one device may be relied on, other than what follows from the above.
Results may differ from a plain program's by a relative error of at most 0.0003.
Values may be sent and summed in bfloat16 or wider, within the bound.
A program may use at most 64 MiB of HBM per device.

v0:
```python
import jax
import jax.numpy as jnp
from jax import lax
from jax.sharding import PartitionSpec as P

NTX = 16
ITERS = 4


storage_coef = 1.0
coupling_coef = 0.25


def shifted(value, axis, steps):
    count = lax.axis_size(axis)
    pairs = [(source, (source + steps) % count) for source in range(count)]
    return lax.ppermute(value, axis, pairs)


def reverse_where(edge_values, reverse_flag):
    return jnp.where(reverse_flag == 1, jnp.flip(edge_values, -1), edge_values)


def attach(field_now, east_edge, west_edge, north_edge, south_edge):
    east_full = jnp.concatenate([field_now[..., 1:], east_edge[..., None]], axis=-1)
    west_full = jnp.concatenate([west_edge[..., None], field_now[..., :-1]], axis=-1)
    north_full = jnp.concatenate([field_now[..., 1:, :], north_edge[..., None, :]], axis=-2)
    south_full = jnp.concatenate([south_edge[..., None, :], field_now[..., :-1, :]], axis=-2)
    return (east_full, west_full, north_full, south_full)


def neighbour_fields(field_now, link_codes):
    east_edge = reverse_where(shifted(field_now[..., :, 0], "tile", -1), link_codes[0])
    west_edge = reverse_where(shifted(field_now[..., :, -1], "tile", 1), link_codes[1])
    north_edge = reverse_where(shifted(field_now[..., 0, :], "tile", -NTX), link_codes[2])
    south_edge = reverse_where(shifted(field_now[..., -1, :], "tile", NTX), link_codes[3])
    return attach(field_now, east_edge, west_edge, north_edge, south_edge)


def column_sum(values, fraction, thickness):
    running = thickness[0] * fraction[0].astype(jnp.float32) * values[:, 0].astype(jnp.float32)
    for level_index in range(1, values.shape[1]):
        running = running + thickness[level_index] * fraction[level_index].astype(
            jnp.float32
        ) * values[:, level_index].astype(jnp.float32)
    return running


def column_depth(fraction, thickness, wet_cells):
    running = thickness[0] * fraction[0].astype(jnp.float32)
    for level_index in range(1, fraction.shape[0]):
        running = running + thickness[level_index] * fraction[level_index].astype(jnp.float32)
    return wet_cells * running


def apply_operator(field_now, diagonal, weights, link_codes):
    east_full, west_full, north_full, south_full = neighbour_fields(field_now, link_codes)
    return (
        diagonal * field_now
        + weights[0] * (field_now - east_full)
        + weights[1] * (field_now - west_full)
        + weights[2] * (field_now - north_full)
        + weights[3] * (field_now - south_full)
    )


def member_sum(first_field, second_field):
    return jnp.sum(first_field * second_field, axis=(1, 2))


def widen(member_values):
    return member_values[:, None, None]


def squares(residual):
    return lax.psum(member_sum(residual, residual), "tile")


def on_device(
    adjoint_zonal, adjoint_meridional, cell_fraction, level_thickness, land_mask, edge_codes
):
    link_codes = edge_codes[0]
    wet_cells = land_mask.astype(jnp.float32)
    water_depth = column_depth(cell_fraction, level_thickness, wet_cells)
    east_values, east_fraction = shifted(
        (adjoint_zonal[..., :, 0], cell_fraction[..., :, 0]), "tile", -1
    )
    north_values, north_fraction = shifted(
        (adjoint_meridional[..., 0, :], cell_fraction[:, 0, :]), "tile", -NTX
    )
    transport_u = column_sum(adjoint_zonal, cell_fraction, level_thickness)
    transport_v = column_sum(adjoint_meridional, cell_fraction, level_thickness)
    east_edge = reverse_where(
        column_sum(east_values, east_fraction, level_thickness), link_codes[0]
    )
    north_edge = reverse_where(
        column_sum(north_values, north_fraction, level_thickness), link_codes[2]
    )
    east_transport = jnp.concatenate([transport_u[..., 1:], east_edge[..., None]], axis=-1)
    north_transport = jnp.concatenate([transport_v[..., 1:, :], north_edge[..., None, :]], axis=-2)
    right_side = wet_cells * (transport_u - east_transport + transport_v - north_transport)
    depth_east, depth_west, depth_north, depth_south = neighbour_fields(water_depth, link_codes)
    weights = (
        coupling_coef * jnp.sqrt(water_depth * depth_east),
        coupling_coef * jnp.sqrt(water_depth * depth_west),
        coupling_coef * jnp.sqrt(water_depth * depth_north),
        coupling_coef * jnp.sqrt(water_depth * depth_south),
    )
    diagonal = storage_coef * wet_cells + (1.0 - wet_cells)
    solution = jnp.zeros_like(right_side)
    residual = right_side
    direction = right_side
    norm_now = squares(residual)
    for step_index in range(ITERS):
        applied = apply_operator(direction, diagonal, weights, link_codes)
        step_size = norm_now / lax.psum(member_sum(direction, applied), "tile")
        solution = solution + widen(step_size) * direction
        residual = residual - widen(step_size) * applied
        norm_next = squares(residual)
        direction = residual + widen(norm_next / norm_now) * direction
        norm_now = norm_next
    return (solution, residual)


def solution(mesh):
    in_specs = (
        P(None, None, "tile", None),
        P(None, None, "tile", None),
        P(None, "tile", None),
        P(),
        P("tile", None),
        P("tile", None),
    )
    out_specs = (P(None, "tile", None), P(None, "tile", None))
    return jax.shard_map(
        on_device, mesh=mesh, in_specs=in_specs, out_specs=out_specs, check_vma=False
    )
```

profile of v0, /device:TPU:1, one launch (start us, length us, event | category | flops | bytes accessed | tf_op | source)
XLA Modules:
  0.0 644.4 jit_solution(16677149107499370670)
XLA Ops:
  0.6 0.7 slice.466
  1.4 0.6 copy.974
  1.9 9.0 %collective-permute-start.2 = (bf16[8,128]{1,0:T(8,128)(2,1)}, bf16[8,128]{1,0:T(8,128)(2,1)S(1)}, u32[]{:S(2)}, u32[]{:S(2)}) collective-permute-start(bf16[8,128]{1,0:T(8,128)(2,1)} %bitcast.348), channel_id=1, source_target_pairs={{0,240},{1,241},{2,242},{3,243},{4,244},{5,245},{6,246},{7,247},{8... | collective-permute-start | bytes 6152 | tf_op jit(solution)/shard_map/ppermute | solution.py:17
  10.9 1.5 copy.890
  12.5 1.0 collective-permute-start
  13.4 0.7 fusion.103
  14.1 0.7 copy-done.5
  14.8 4.9 subtract_add_fusion
  19.7 0.7 slice_reduce_fusion.5
  20.4 2.4 collective-permute-start.4
  22.8 0.6 slice_bitcast_fusion.25
  23.4 1.9 collective-permute-start.8
  25.3 4.9 fusion.80
  30.2 1.1 slice.468
  31.4 1.6 fusion.90
  33.0 0.7 fusion.102
  36.4 1.2 copy.891
  38.4 0.7 copy-done.2
  39.1 0.7 copy-done.8
  39.7 1.1 collective-permute-start.10
  40.9 0.7 rev.72
  41.6 1.5 collective-permute-start.1
  43.1 0.8 rev.74
  44.1 4.6 collective-permute-start.3
  48.7 4.9 multiply_bitcast_fusion.20
  53.6 0.8 rev.76
  54.4 0.7 fusion.83
  55.2 4.9 multiply_bitcast_fusion.12
  60.6 0.5 copy-done.3
  62.1 4.2 collective-permute-start.5
  66.3 1.9 collective-permute-start.9
  68.2 1.4 collective-permute-start.11
  69.9 0.7 collective-permute-done.9
  70.7 3.6 collective-permute-done.11
  74.5 0.4 multiply_reduce_fusion.6
  74.9 78.3 %all-reduce = (f32[32]{0:T(128)S(1)}, f32[32]{0:T(128)S(1)}) all-reduce(f32[32]{0:T(128)S(1)} %get-tuple-element.11, f32[32]{0:T(128)S(1)} %get-tuple-element.10), channel_id=1, replica_groups=mesh['tile'=256] {'tile'}, use_global_device_ids=true, to_apply=%region_1.2 | all-reduce | flops 64 | bytes 512 | tf_op jit(solution)/shard_map/psum | solution.py:76
  153.4 72.8 %psum.58 = f32[32]{0:T(128)S(1)} all-reduce(f32[32]{0:T(128)S(1)} %multiply_reduce_fusion.5), channel_id=1, replica_groups=mesh['tile'=256] {'tile'}, use_global_device_ids=true, to_apply=%region_5.6 | all-reduce | flops 32 | bytes 256 | tf_op jit(solution)/shard_map/psum | solution.py:76
  226.9 1.8 collective-permute-start.13
  228.7 2.0 collective-permute-start.14
  230.7 0.9 collective-permute-start.15
  232.1 0.6 collective-permute-done.14
  232.9 4.1 collective-permute-done.15
  237.0 0.4 multiply_reduce_fusion.4
  237.4 77.0 %psum.59 = f32[32]{0:T(128)S(1)} all-reduce(f32[32]{0:T(128)S(1)} %get-tuple-element.24), channel_id=1, replica_groups=mesh['tile'=256] {'tile'}, use_global_device_ids=true, to_apply=%region_7.8 | all-reduce | flops 32 | bytes 256 | tf_op jit(solution)/shard_map/psum | solution.py:116
  314.7 73.4 %psum.60 = f32[32]{0:T(128)S(1)} all-reduce(f32[32]{0:T(128)S(1)} %get-tuple-element.22), channel_id=1, replica_groups=mesh['tile'=256] {'tile'}, use_global_device_ids=true, to_apply=%region_9.10 | all-reduce | flops 32 | bytes 256 | tf_op jit(solution)/shard_map/psum | solution.py:76
  389.1 1.4 collective-permute-start.17
  390.5 2.0 collective-permute-start.18
  392.6 0.9 collective-permute-start.19
  394.0 3.3 collective-permute-done.16
  397.8 1.4 collective-permute-done.19
  399.3 0.4 multiply_reduce_fusion.2
  399.7 82.3 %psum.61 = f32[32]{0:T(128)S(1)} all-reduce(f32[32]{0:T(128)S(1)} %get-tuple-element.20), channel_id=1, replica_groups=mesh['tile'=256] {'tile'}, use_global_device_ids=true, to_apply=%region_11.12 | all-reduce | flops 32 | bytes 256 | tf_op jit(solution)/shard_map/psum | solution.py:116
  482.0 0.5 multiply_reduce_fusion.1
  482.5 72.4 %psum.62 = f32[32]{0:T(128)S(1)} all-reduce(f32[32]{0:T(128)S(1)} %get-tuple-element.18), channel_id=1, replica_groups=mesh['tile'=256] {'tile'}, use_global_device_ids=true, to_apply=%region_13.14 | all-reduce | flops 32 | bytes 256 | tf_op jit(solution)/shard_map/psum | solution.py:76
  555.6 0.7 collective-permute-start.20
  556.3 2.6 collective-permute-start.22
  558.9 0.4 collective-permute-start.23
  559.5 1.7 collective-permute-start.21
  561.2 1.9 collective-permute-done.21
  563.6 0.7 slice-done
  564.5 0.6 collective-permute-done.23
  565.2 0.3 multiply_reduce_fusion
  565.5 77.7 %psum.63 = f32[32]{0:T(128)S(1)} all-reduce(f32[32]{0:T(128)S(1)} %multiply_reduce_fusion), channel_id=1, replica_groups=mesh['tile'=256] {'tile'}, use_global_device_ids=true, to_apply=%region_15.16 | all-reduce | flops 32 | bytes 256 | tf_op jit(solution)/shard_map/psum | solution.py:116
  643.2 1.2 multiply_subtract_fusion
  (135 shorter events, 8.7 us)
Async XLA Ops:
  1.9 53.3 %collective-permute-start.2 = (bf16[8,128]{1,0:T(8,128)(2,1)}, bf16[8,128]{1,0:T(8,128)(2,1)S(1)}, u32[]{:S(2)}, u32[]{:S(2)}) collective-permute-start(bf16[8,128]{1,0:T(8,128)(2,1)} %bitcast.348), channel_id=1, source_target_pairs={{0,240},{1,241},{2,242},{3,243},{4,244},{5,245},{6,246},{7,247},{8... | collective-permute-start | bytes 6152 | tf_op jit(solution)/shard_map/ppermute | solution.py:17
  10.9 3.1 copy-start.4
  12.5 1.0 copy-start.6
  12.5 31.6 %collective-permute-start = (bf16[8,16]{1,0:T(8,128)(2,1)}, bf16[8,16]{1,0:T(8,128)(2,1)S(1)}, u32[]{:S(2)}, u32[]{:S(2)}) collective-permute-start(bf16[8,16]{1,0:T(8,128)(2,1)} %bitcast.25), channel_id=1, source_target_pairs={{0,255},{1,0},{2,1},{3,2},{4,3},{5,4},{6,5},{7,6},{8,7},{9,8},{10,... | collective-permute-start | bytes 776 | tf_op jit(solution)/shard_map/ppermute | solution.py:17
  14.1 0.7 copy-start.5
  20.4 18.7 %collective-permute-start.4 = (f32[16]{0:T(128)}, f32[16]{0:T(128)}, u32[]{:S(2)}, u32[]{:S(2)}) collective-permute-start(f32[16]{0:T(128)} %get-tuple-element.14), channel_id=1, source_target_pairs={{0,255},{1,0},{2,1},{3,2},{4,3},{5,4},{6,5},{7,6},{8,7},{9,8},{10,... | collective-permute-start | bytes 200 | tf_op jit(solution)/shard_map/ppermute | solution.py:17
  22.8 18.8 %collective-permute-start.6 = (f32[16]{0:T(128)}, f32[16]{0:T(128)}, u32[]{:S(2)}, u32[]{:S(2)}) collective-permute-start(f32[16]{0:T(128)} %get-tuple-element.15), channel_id=1, source_target_pairs={{0,1},{1,2},{2,3},{3,4},{4,5},{5,6},{6,7},{7,8},{8,9},{9,10},{10,1... | collective-permute-start | bytes 200 | tf_op jit(solution)/shard_map/ppermute | solution.py:17
  23.4 30.2 %collective-permute-start.8 = (f32[128]{0:T(128)}, f32[128]{0:T(128)}, u32[]{:S(2)}, u32[]{:S(2)}) collective-permute-start(f32[128]{0:T(128)} %get-tuple-element.90), channel_id=1, source_target_pairs={{0,240},{1,241},{2,242},{3,243},{4,244},{5,245},{6,246},{7,247},{8... | collective-permute-start | bytes 1544 | tf_op jit(solution)/shard_map/ppermute | solution.py:17
  31.3 1.6 copy-start.7
  31.4 4.8 copy-start.1
  38.4 0.7 copy-start.2
  39.1 0.7 copy-start.8
  39.7 14.6 %collective-permute-start.10 = (f32[128]{0:T(128)S(1)}, f32[128]{0:T(128)S(1)}, u32[]{:S(2)}, u32[]{:S(2)}) collective-permute-start(f32[128]{0:T(128)S(1)} %copy-done.8), channel_id=1, source_target_pairs={{0,16},{1,17},{2,18},{3,19},{4,20},{5,21},{6,22},{7,23},{8,24},{9,... | collective-permute-start | bytes 1544 | tf_op jit(solution)/shard_map/ppermute | solution.py:17
  41.6 18.5 %collective-permute-start.1 = (bf16[32,8,16]{0,2,1:T(8,128)(2,1)S(1)}, bf16[32,8,16]{0,2,1:T(8,128)(2,1)S(1)}, u32[]{:S(2)}, u32[]{:S(2)}) collective-permute-start(bf16[32,8,16]{0,2,1:T(8,128)(2,1)S(1)} %bitcast.359), channel_id=1, source_target_pairs={{0,255},{1,0},{2,1},{3,2},{4,3},{5,4},{6,5},{7,6},{8,7},{9,8},{10,... | collective-permute-start | bytes 24584 | tf_op jit(solution)/shard_map/ppermute | solution.py:17
  44.1 16.4 %collective-permute-start.3 = (bf16[32,8,128]{2,0,1:T(8,128)(2,1)S(1)}, bf16[32,8,128]{2,0,1:T(8,128)(2,1)S(1)}, u32[]{:S(2)}, u32[]{:S(2)}) collective-permute-start(bf16[32,8,128]{2,0,1:T(8,128)(2,1)S(1)} %bitcast.358), channel_id=1, source_target_pairs={{0,240},{1,241},{2,242},{3,243},{4,244},{5,245},{6,246},{7,247},{8... | collective-permute-start | bytes 196616 | tf_op jit(solution)/shard_map/ppermute | solution.py:17
  60.2 1.0 copy-start.3
  60.3 1.0 slice-start.1
  62.0 7.5 %collective-permute-start.7 = (f32[32,16]{0,1:T(8,128)S(1)}, f32[32,16]{0,1:T(8,128)S(1)}, u32[]{:S(2)}, u32[]{:S(2)}) collective-permute-start(f32[32,16]{0,1:T(8,128)S(1)} %get-tuple-element.12), channel_id=1, source_target_pairs={{0,1},{1,2},{2,3},{3,4},{4,5},{5,6},{6,7},{7,8},{8,9},{9,10},{10,1... | collective-permute-start | bytes 6152 | tf_op jit(solution)/shard_map/ppermute | solution.py:17
  62.1 7.5 %collective-permute-start.5 = (f32[32,16]{0,1:T(8,128)S(1)}, f32[32,16]{0,1:T(8,128)S(1)}, u32[]{:S(2)}, u32[]{:S(2)}) collective-permute-start(f32[32,16]{0,1:T(8,128)S(1)} %get-tuple-element.13), channel_id=1, source_target_pairs={{0,255},{1,0},{2,1},{3,2},{4,3},{5,4},{6,5},{7,6},{8,7},{9,8},{10,... | collective-permute-start | bytes 6152 | tf_op jit(solution)/shard_map/ppermute | solution.py:17
  66.3 4.4 collective-permute-start.9
  68.2 6.2 collective-permute-start.11
  226.9 4.8 collective-permute-start.13
  228.7 3.1 collective-permute-start.12
  228.7 4.1 collective-permute-start.14
  230.7 6.2 collective-permute-start.15
  389.1 4.8 collective-permute-start.17
  390.5 7.2 %collective-permute-start.18 = (f32[32,128]{1,0:T(8,128)S(1)}, f32[32,128]{1,0:T(8,128)S(1)}, u32[]{:S(2)}, u32[]{:S(2)}) collective-permute-start(f32[32,128]{1,0:T(8,128)S(1)} %get-tuple-element.58), channel_id=1, source_target_pairs={{0,240},{1,241},{2,242},{3,243},{4,244},{5,245},{6,246},{7,247},{8... | collective-permute-start | bytes 49160 | tf_op jit(solution)/shard_map/ppermute | solution.py:17
  392.6 6.6 %collective-permute-start.19 = (f32[32,128]{1,0:T(8,128)S(1)}, f32[32,128]{1,0:T(8,128)S(1)}, u32[]{:S(2)}, u32[]{:S(2)}) collective-permute-start(f32[32,128]{1,0:T(8,128)S(1)} %get-tuple-element.59), channel_id=1, source_target_pairs={{0,16},{1,17},{2,18},{3,19},{4,20},{5,21},{6,22},{7,23},{8,24},{9,... | collective-permute-start | bytes 49160 | tf_op jit(solution)/shard_map/ppermute | solution.py:17
  393.7 3.6 collective-permute-start.16
  555.1 1.2 copy-start
  555.6 5.6 collective-permute-start.20
  556.3 7.2 %collective-permute-start.22 = (f32[32,128]{1,0:T(8,128)S(1)}, f32[32,128]{1,0:T(8,128)S(1)}, u32[]{:S(2)}, u32[]{:S(2)}) collective-permute-start(f32[32,128]{1,0:T(8,128)S(1)} %get-tuple-element.46), channel_id=1, source_target_pairs={{0,240},{1,241},{2,242},{3,243},{4,244},{5,245},{6,246},{7,247},{8... | collective-permute-start | bytes 49160 | tf_op jit(solution)/shard_map/ppermute | solution.py:17
  558.9 6.2 collective-permute-start.23
  559.5 3.6 collective-permute-start.21
  563.3 0.9 slice-start
where the time goes:
time: 647 us; the launch traced here: 644 us
  blocking collectives  534 us (83%)
  starting transfers between devices  43.8 us (7%)
  other arithmetic  26 us (4%)
  local copies, waits for them, and re-layouts  20.6 us (3%)
  waiting for transfers between devices  16.5 us (3%)
    psum x4, blocking collectives, squares(): return lax.psum(member_sum(residual, residual), 'tile')  297 us
    psum x3, blocking collectives, on_device(): step_size = norm_now / lax.psum(member_sum(direction, applied), 'tile')  237 us
    ppermute x24, starting transfers between devices, shifted(): return lax.ppermute(value, axis, pairs)  43.8 us
    ppermute x24, waiting for transfers between devices, shifted(): return lax.ppermute(value, axis, pairs)  16.5 us
    mul x3, other arithmetic, column_sum(): thickness[0] * fraction[0].astype(jnp.float32)  14.6 us
  transfers between devices with their start and end apart: 24, of which 9 were waited for; matrix products, arithmetic and copies ran while one was open for 5% of the time, Pallas kernels for 0%

commit v1 on v0

v1 whole, which is shorter than its diff:
```python
import functools

import jax
import jax.numpy as jnp
from jax import lax
from jax.experimental import pallas as pl
from jax.experimental.pallas import tpu as pltpu
from jax.sharding import PartitionSpec as P

MESH = pl.DeviceIdType.MESH
F32 = jnp.float32
MEMB, LEV, TY, TX = 32, 8, 16, 128
NTX = 16
PLANE, DEPTH = 32, 8
N_TILE = PLANE * DEPTH
PITCH = 48
UNROLL = 4
CHUNKS = 4


def lanes(shape):
    return lax.broadcasted_iota(jnp.int32, shape, len(shape) - 1)


def roll_lanes(x, shift):
    return pltpu.roll(x, shift % 128, axis=x.ndim - 1)


def exchange_groups(a):
    lane = lanes(a[0].shape)
    low = lane < 64
    even = (lane // 32) % 2 == 0
    b0 = jnp.where(low, a[0], roll_lanes(a[2], 64))
    b2 = jnp.where(low, roll_lanes(a[0], 64), a[2])
    b1 = jnp.where(low, a[1], roll_lanes(a[3], 64))
    b3 = jnp.where(low, roll_lanes(a[1], 64), a[3])
    return (
        jnp.where(even, b0, roll_lanes(b1, 32)),
        jnp.where(even, roll_lanes(b0, 96), b1),
        jnp.where(even, b2, roll_lanes(b3, 32)),
        jnp.where(even, roll_lanes(b2, 96), b3),
    )


def reverse8(x):
    place = lax.broadcasted_iota(jnp.int32, x.shape, 0)
    x = pltpu.roll(x, 4, axis=0)
    x = jnp.where(place % 4 < 2, pltpu.roll(x, 6, axis=0), pltpu.roll(x, 2, axis=0))
    return jnp.where(place % 2 < 1, pltpu.roll(x, 7, axis=0), pltpu.roll(x, 1, axis=0))


def reverse_rows(x):
    blocks = x.shape[0] // 8
    return jnp.concatenate(
        [reverse8(x[8 * k : 8 * k + 8]) for k in range(blocks - 1, -1, -1)], axis=0
    )


def reverse_columns(x):
    even = (lanes(x.shape) // 32) % 2 == 0
    return reverse_rows(jnp.where(even, roll_lanes(x, 32), roll_lanes(x, 96)))


def pack_sums(p):
    p = [x[0:8] + x[8:16] + (x[16:24] + x[24:32]) for x in p]
    lane = lanes(p[0].shape)
    low = lane < 64
    even = (lane // 32) % 2 == 0
    x = jnp.where(low, p[0] + roll_lanes(p[0], 64), p[2] + roll_lanes(p[2], 64))
    y = jnp.where(low, p[1] + roll_lanes(p[1], 64), p[3] + roll_lanes(p[3], 64))
    z = jnp.where(even, x + roll_lanes(x, 96), y + roll_lanes(y, 32))
    return jnp.sum(z, axis=0, keepdims=True)


def spread(row):
    lane = lanes(row.shape)
    out = []
    for k in range(4):
        x = jnp.where(lane // 32 == k, row, 0.0)
        x = x + roll_lanes(x, 64)
        out.append(x + roll_lanes(x, 32))
    return out


def kernel(
    u_hbm, v_hbm, fraction, thickness, land, codes, x_out, r_out,
    u_buf, v_buf, tu1, tv1, weight, tu2, tv2, field, g_buf, q_buf, qsum, stage,
    edge_send, edge_recv, tu_send, tu_recv, tv_send, tv_recv, a1, b1, a2, b2,
    load_sem, send_sem, recv_sem, ar_send, ar_recv,
):
    me = lax.axis_index("tile")
    east, west = lax.rem(me + 1, N_TILE), lax.rem(me + N_TILE - 1, N_TILE)
    north, south = lax.rem(me + NTX, N_TILE), lax.rem(me + N_TILE - NTX, N_TILE)
    level, place = me // PLANE, lax.rem(me, PLANE)
    plane_peers = [level * PLANE + lax.rem(place + d, PLANE) for d in range(1, PLANE)]
    level_peers = [lax.rem(level + d, DEPTH) * PLANE + place for d in range(1, DEPTH)]

    part = MEMB // CHUNKS
    loads = []
    for c in range(CHUNKS):
        for n, (src, dst) in enumerate(((u_hbm, u_buf), (v_hbm, v_buf))):
            at = pl.ds(c * part, part)
            copy = pltpu.make_async_copy(src.at[at], dst.at[at], load_sem.at[n, c])
            copy.start()
            loads.append(copy)

    barrier = pltpu.get_barrier_semaphore()
    greeted = [east, west, north, south] + plane_peers + level_peers
    for peer in greeted:
        pl.semaphore_signal(barrier, inc=1, device_id=(peer,), device_id_type=MESH)

    flip = [codes[0, k] == 1 for k in range(4)]

    depth = None
    for k in range(LEV):
        w = thickness[k] * fraction[k].astype(F32)
        weight[k] = w
        depth = w if depth is None else depth + w
    root = 0.5 * jnp.sqrt(land[...].astype(F32) * depth)
    stage[...] = root

    def to_groups(rows_of, store):
        for block in range(4):
            z = jnp.concatenate([rows_of(4 * block + k) for k in range(4)], axis=0)
            t = jnp.transpose(z)
            out = exchange_groups([t[32 * g : 32 * g + 32] for g in range(4)])
            for k in range(4):
                store(4 * block + k, out[k])

    def inner(i):
        start = (i + 1) * PITCH + 8
        if not isinstance(i, int):
            start = pl.multiple_of(start, 8)
        return pl.ds(start, 32)

    def column(s):
        return pl.ds(PITCH + 8 + s, TY, stride=PITCH)

    def store_q(i, value):
        q_buf[i] = value
        g_buf[0, inner(i), :] = value

    to_groups(lambda i: jnp.broadcast_to(stage[pl.ds(i, 1), :], (MEMB, TX)), store_q)

    def column_sums(src, dst, n):
        for c in range(CHUNKS):
            loads[2 * c + n].wait()

            def member(m, carry):
                total = weight[0] * src[m, 0].astype(F32)
                for k in range(1, LEV):
                    total = total + weight[k] * src[m, k].astype(F32)
                dst[pl.ds(pl.multiple_of(m * TY, TY), TY), :] = total
                return carry

            lax.fori_loop(c * part, (c + 1) * part, member, 0, unroll=2)

    def remote(src, dst, index, direction, peer):
        return pltpu.make_async_remote_copy(
            src_ref=src, dst_ref=dst,
            send_sem=send_sem.at[index, direction], recv_sem=recv_sem.at[index, direction],
            device_id=(peer,), device_id_type=MESH,
        )

    def edges(k):
        return [
            remote(edge_send.at[k, 2], g_buf.at[k, pl.ds(17 * PITCH + 8, 32)], k, 2, south),
            remote(edge_send.at[k, 3], g_buf.at[k, pl.ds(8, 32)], k, 3, north),
            remote(edge_send.at[k, 0, pl.ds(0, TY)], edge_recv.at[k, 0], k, 0, west),
            remote(edge_send.at[k, 1, pl.ds(0, TY)], edge_recv.at[k, 1], k, 1, east),
        ]

    def put_rows(k):
        low, high = g_buf[k, inner(0), :], g_buf[k, inner(TY - 1), :]
        edge_send[k, 2] = jnp.where(flip[3], reverse_columns(low), low)
        edge_send[k, 3] = jnp.where(flip[2], reverse_columns(high), high)

    def put_columns(k):
        first, last = g_buf[k, column(0), :], g_buf[k, column(31), :]
        to_west = roll_lanes(first, 96)
        to_east = roll_lanes(last, 32)
        edge_send[k, 0, pl.ds(0, TY)] = jnp.where(flip[1], reverse_rows(to_west), to_west)
        edge_send[k, 1, pl.ds(0, TY)] = jnp.where(flip[0], reverse_rows(to_east), to_east)
        return to_west, to_east

    def take_columns(k, to_west, to_east):
        lane = lanes(to_west.shape)
        g_buf[k, column(32), :] = jnp.where(lane < 96, to_west, edge_recv[k, 0])
        g_buf[k, column(-1), :] = jnp.where(lane >= 32, to_east, edge_recv[k, 1])

    sent = []

    def send_edges(k):
        put_rows(k)
        copies = edges(k)
        copies[0].start()
        copies[1].start()
        own = put_columns(k)
        copies[2].start()
        copies[3].start()
        sent.extend(copies)
        return copies, own

    def take_edges(k, copies, own):
        copies[2].wait_recv()
        copies[3].wait_recv()
        take_columns(k, *own)
        copies[0].wait_recv()
        copies[1].wait_recv()

    def around(k, i):
        here = inner(i)
        base = here.start
        return (g_buf[k, pl.ds(base + 1, 32), :] + g_buf[k, pl.ds(base - 1, 32), :]) + (
            g_buf[k, inner(i + 1), :] + g_buf[k, inner(i - 1), :]
        )

    column_sums(u_buf, tu1, 0)
    column_sums(v_buf, tv1, 1)

    def store_tu(i, value):
        tu2[inner(i), :] = value

    def store_tv(i, value):
        tv2[pl.ds(i * 32, 32), :] = value

    to_groups(lambda i: tv1[pl.ds(i, MEMB, stride=TY), :], store_tv)
    to_groups(lambda i: tu1[pl.ds(i, MEMB, stride=TY), :], store_tu)

    row = tv2[pl.ds(0, 32), :]
    tv_send[...] = jnp.where(flip[3], reverse_columns(row), row)
    own_tu = roll_lanes(tu2[column(0), :], 96)
    tu_send[...] = jnp.where(flip[1], reverse_rows(own_tu), own_tu)

    pl.semaphore_wait(barrier, len(greeted))
    tv_copy = remote(tv_send, tv2.at[pl.ds(TY * 32, 32)], 5, 2, south)
    tv_copy.start()
    tu_copy = remote(tu_send, tu_recv, 5, 0, west)
    tu_copy.start()
    copies, own = send_edges(0)
    tu_copy.wait_recv()
    tu2[column(32), :] = jnp.where(lanes(own_tu.shape) < 96, own_tu, tu_recv[...])
    tv_copy.wait_recv()
    take_edges(0, copies, own)

    zero = jnp.zeros((32, 128), F32)

    def first(i, total):
        q = q_buf[i]
        here = inner(i)
        below = pl.multiple_of(i * 32, 32)
        value = (
            tu2[here, :] - tu2[pl.ds(here.start + 1, 32), :]
            + tv2[pl.ds(below, 32), :] - tv2[pl.ds(below + 32, 32), :]
        )
        value = jnp.where(q > 0.0, value, 0.0)
        qsum[i] = around(0, i)
        field[0, i] = value
        g_buf[1, here, :] = q * value
        return total + value * value

    n0 = lax.fori_loop(0, TY, first, zero, unroll=UNROLL)

    def image(k, square):
        copies, own = send_edges(k)
        yield
        take_edges(k, copies, own)

        def step(i, totals):
            q, old = q_buf[i], field[k - 1, i]
            value = q * (qsum[i] * old - around(k, i))
            field[k, i] = value
            if k < 4:
                g_buf[k + 1, inner(i), :] = q * value
            if square is None:
                return totals
            cross, own_square = totals
            return cross + old * value, own_square + value * value if square else own_square

        yield lax.fori_loop(0, TY, step, (zero, zero), unroll=UNROLL)

    def make_image(k, square, between=None):
        steps = image(k, square)
        next(steps)
        if between is not None:
            between()
        return next(steps)

    def fan(buf, slot, peers, phase, which):
        def copy_to(peer):
            return pltpu.make_async_remote_copy(
                src_ref=buf.at[slot], dst_ref=buf.at[slot],
                send_sem=ar_send.at[which, phase], recv_sem=ar_recv.at[which, phase],
                device_id=(peer,), device_id_type=MESH,
            )

        for peer in peers:
            copy_to(peer).start()

    def fan_wait(buf, count, sem):
        pltpu.make_async_copy(buf.at[pl.ds(0, count)], buf.at[pl.ds(0, count)], sem).wait()

    def start_level(values, buf, which):
        buf[place] = values
        fan(buf, place, plane_peers, 0, which)

    def cross_levels(buf_a, buf_b, which):
        fan_wait(buf_a, PLANE - 1, ar_recv.at[which, 0])
        buf_b[level] = jnp.sum(buf_a[...], axis=0)
        fan(buf_b, level, level_peers, 1, which)

    def finish(buf_b, which):
        fan_wait(buf_b, DEPTH - 1, ar_recv.at[which, 1])
        return jnp.sum(buf_b[...], axis=0)

    n1, n2 = make_image(1, True)
    n3, _ = make_image(2, False)
    make_image(3, None, lambda: start_level(pack_sums([n0, n1, n2, n3]), a1, 0))
    make_image(4, None, lambda: cross_levels(a1, b1, 0))
    s0, s1, s2, s3 = spread(finish(b1, 0))

    m0, m1, m2, m3 = s0, s0 + s1, s0 + 2.0 * s1 + s2, s0 + 3.0 * (s1 + s2) + s3
    alpha0 = m0 / m1
    rr1 = m0 - alpha0 * (2.0 * m1 - alpha0 * m2)
    gain = 1.0 + rr1 / m0
    alpha1 = rr1 / (gain * gain * m1 - alpha0 * (2.0 * gain * m2 - alpha0 * m3))
    lead = alpha0 * alpha1
    lin = -(alpha0 + alpha1 * gain)
    c0, c1, c2 = 1.0 + lin + lead, lin + 2.0 * lead, lead
    e0, e1 = gain - alpha0, -alpha0
    x0, x1 = -lin - lead, -lead

    def rows(*values):
        return [jnp.broadcast_to(v, (32, 128)) for v in values]

    c0b, c1b, c2b, e0b, e1b = rows(c0, c1, c2, e0, e1)

    def second(i, totals):
        v = [field[k, i] for k in range(5)]
        r = [c0b * v[k] + c1b * v[k + 1] + c2b * v[k + 2] for k in range(3)]
        d = [e0b * v[k] + e1b * v[k + 1] for k in range(3)]
        here = inner(i)
        for k in range(3):
            g_buf[k, here, :] = r[k]
        g_buf[3, here, :] = d[0]
        g_buf[4, here, :] = d[1]
        tu2[here, :] = d[2]
        pairs = (
            (r[0], r[0]), (r[0], d[0]), (d[0], d[0]), (r[0], r[1]),
            (r[0], d[1]), (d[0], d[1]), (r[1], r[1]), (r[1], d[1]),
            (d[1], d[1]), (r[1], r[2]), (r[1], d[2]), (d[1], d[2]),
        )
        out = []
        for t, (x, y) in zip(totals, pairs):
            p = x * y
            out.append(t + (p[0:8] + p[8:16] + (p[16:24] + p[24:32])))
        return tuple(out)

    small = jnp.zeros((8, 128), F32)
    totals = lax.fori_loop(0, TY, second, (small,) * 12, unroll=2)
    wide = [jnp.concatenate([t, jnp.zeros((24, 128), F32)], axis=0) for t in totals]
    packed = [pack_sums(wide[4 * k : 4 * k + 4]) for k in range(3)]
    start_level(jnp.concatenate(packed + [packed[0] * 0.0], axis=0), a2, 1)
    cross_levels(a2, b2, 1)
    sums = finish(b2, 1)
    rr, rd, dd, rr_1 = spread(sums[0:1])
    rd_1, dd_1, rr_2, rd_2 = spread(sums[1:2])
    dd_2, rr_3, rd_3, dd_3 = spread(sums[2:3])
    r1 = rr + rr_1
    r2 = rr + 2.0 * rr_1 + rr_2
    r3 = rr + 3.0 * (rr_1 + rr_2) + rr_3
    y1 = rd + rd_1
    y2 = rd + 2.0 * rd_1 + rd_2
    y3 = rd + 3.0 * (rd_1 + rd_2) + rd_3
    d1 = dd + dd_1
    d2 = dd + 2.0 * dd_1 + dd_2
    d3 = dd + 3.0 * (dd_1 + dd_2) + dd_3
    beta1 = rr / rr1
    p1 = r1 + beta1 * (2.0 * y1 + beta1 * d1)
    p2 = r2 + beta1 * (2.0 * y2 + beta1 * d2)
    p3 = r3 + beta1 * (2.0 * y3 + beta1 * d3)
    rp1 = r1 + beta1 * y1
    rp2 = r2 + beta1 * y2
    alpha2 = rr / p1
    rr3 = rr - alpha2 * (2.0 * rp1 - alpha2 * p2)
    beta2 = rr3 / rr
    q1 = (
        r1 + alpha2 * (alpha2 * p3 - 2.0 * rp2)
        + beta2 * (2.0 * (rp1 - alpha2 * p2) + beta2 * p1)
    )
    alpha3 = rr3 / q1
    kappa = alpha2 + alpha3 * beta2
    mu = alpha2 * alpha3
    xp0 = kappa - mu
    xr0, xr1 = xp0 + alpha3, -mu
    xd0, xd1 = beta1 * xp0, -beta1 * mu
    fp0, fp1, fp2 = mu - kappa, 2.0 * mu - kappa, mu
    fr0, fr1, fr2 = 1.0 + fp0 - alpha3, fp1 - alpha3, fp2
    fd0, fd1, fd2 = beta1 * fp0, beta1 * fp1, beta1 * fp2
    cx = rows(x0, x1, xr0, xr1, xd0, xd1)
    cr = rows(fr0, fr1, fr2, fd0, fd1, fd2)

    for block in range(4):
        xs, rs = [], []
        for k in range(4):
            i = 4 * block + k
            here = inner(i)
            r = [g_buf[n, here, :] for n in range(3)]
            d = [g_buf[3, here, :], g_buf[4, here, :], tu2[here, :]]
            parts = (field[0, i], field[1, i], r[0], r[1], d[0], d[1])
            xs.append(functools.reduce(lambda s, t: s + t, [c * t for c, t in zip(cx, parts)]))
            rs.append(functools.reduce(lambda s, t: s + t, [c * t for c, t in zip(cr, r + d)]))
        for values, out in ((xs, x_out), (rs, r_out)):
            t = jnp.transpose(jnp.concatenate(exchange_groups(values), axis=0))
            for k in range(4):
                out[pl.ds(4 * block + k, MEMB, stride=TY), :] = t[32 * k : 32 * k + 32]

    for copy in sent + [tv_copy, tu_copy]:
        copy.wait_send()
    fan_wait(a1, PLANE - 1, ar_send.at[0, 0])
    fan_wait(b1, DEPTH - 1, ar_send.at[0, 1])
    fan_wait(a2, PLANE - 1, ar_send.at[1, 0])
    fan_wait(b2, DEPTH - 1, ar_send.at[1, 1])


def on_device(zonal, meridional, fraction, thickness, land, codes):
    vmem = pl.BlockSpec(memory_space=pltpu.VMEM)
    smem = pl.BlockSpec(memory_space=pltpu.SMEM)
    hbm = pl.BlockSpec(memory_space=pl.ANY)
    flat = jax.ShapeDtypeStruct((MEMB * TY, TX), F32)
    padded = (TY + 2) * PITCH
    x, r = pl.pallas_call(
        kernel,
        out_shape=(flat, flat),
        in_specs=[hbm, hbm, vmem, smem, vmem, smem],
        out_specs=(vmem, vmem),
        scratch_shapes=[
            pltpu.VMEM((MEMB, LEV, TY, TX), jnp.bfloat16),
            pltpu.VMEM((MEMB, LEV, TY, TX), jnp.bfloat16),
            pltpu.VMEM((MEMB * TY, TX), F32),
            pltpu.VMEM((MEMB * TY, TX), F32),
            pltpu.VMEM((LEV, TY, TX), F32),
            pltpu.VMEM((padded, 128), F32),
            pltpu.VMEM(((TY + 1) * 32, 128), F32),
            pltpu.VMEM((5, TY, 32, 128), F32),
            pltpu.VMEM((5, padded, 128), F32),
            pltpu.VMEM((TY, 32, 128), F32),
            pltpu.VMEM((TY, 32, 128), F32),
            pltpu.VMEM((TY, TX), F32),
            pltpu.VMEM((5, 4, 32, 128), F32),
            pltpu.VMEM((5, 2, TY, 128), F32),
            pltpu.VMEM((TY, 128), F32),
            pltpu.VMEM((TY, 128), F32),
            pltpu.VMEM((32, 128), F32),
            pltpu.VMEM((32, 128), F32),
            pltpu.VMEM((PLANE, 1, 128), F32),
            pltpu.VMEM((DEPTH, 1, 128), F32),
            pltpu.VMEM((PLANE, 4, 128), F32),
            pltpu.VMEM((DEPTH, 4, 128), F32),
            pltpu.SemaphoreType.DMA((2, CHUNKS)),
            pltpu.SemaphoreType.DMA((6, 4)),
            pltpu.SemaphoreType.DMA((6, 4)),
            pltpu.SemaphoreType.DMA((2, 2)),
            pltpu.SemaphoreType.DMA((2, 2)),
        ],
        compiler_params=pltpu.CompilerParams(
            collective_id=0, has_side_effects=True, vmem_limit_bytes=40 << 20
        ),
    )(zonal, meridional, fraction, thickness, land, codes)
    return x.reshape(MEMB, TY, TX), r.reshape(MEMB, TY, TX)


def solution(mesh):
    in_specs = (
        P(None, None, "tile", None),
        P(None, None, "tile", None),
        P(None, "tile", None),
        P(),
        P("tile", None),
        P("tile", None),
    )
    out_specs = (P(None, "tile", None), P(None, "tile", None))
    return jax.shard_map(
        on_device, mesh=mesh, in_specs=in_specs, out_specs=out_specs, check_vma=False
    )
```

time: 647 us -> 55.3 us (0.09)
  blocking collectives: 534 us -> 0 us
  Pallas kernels: 0 us -> 47.8 us
  starting transfers between devices: 43.8 us -> 0 us
  other arithmetic: 26 us -> 0 us
  waiting for transfers between devices: 16.5 us -> 0 us
  local copies, waits for them, and re-layouts: 20.6 us -> 6.61 us
    psum x7 -> x0, blocking collectives: 534 us -> none  [the longest x4 297 us: squares(): return lax.psum(member_sum(residual, residual), 'tile')]
    pallas_call x0 -> x1, Pallas kernels: none -> 47.8 us  [on_device(): pl.pallas_call(kernel, out_shape=(flat, flat), in_specs=[hbm, hbm, vmem,...]
    ppermute x24 -> x0, starting transfers between devices: 43.8 us -> none  [shifted(): return lax.ppermute(value, axis, pairs)]
    ppermute x24 -> x0, waiting for transfers between devices: 16.5 us -> none  [shifted(): return lax.ppermute(value, axis, pairs)]
    mul x6 -> x0, other arithmetic: 15 us -> none  [the longest x3 14.6 us: column_sum(): thickness[0] * fraction[0].astype(jnp.float32)]
    slice x29 -> x0, local copies, waits for them, and re-layouts: 8.99 us -> none  [the longest x2 1.77 us: column_sum(): values[:, 0].astype(jnp.float32)]
  transfers between devices with their start and end apart: 24 -> 0, of which waited for: 9 -> 0; matrix products, arithmetic and copies ran while one was open for 5% -> 0% of each run, Pallas kernels for 0% -> 0%
where the time goes in v1:
time: 55.3 us; the launch traced here: 55 us
  Pallas kernels  47.8 us (86%)
  local copies, waits for them, and re-layouts  6.61 us (12%)
  between operations  0.65 us (1%)
    pallas_call x1, Pallas kernels, on_device(): pl.pallas_call(kernel, out_shape=(flat, flat), in_specs=[hbm, hbm, vmem,...  47.8 us
    unnamed x14, local copies, waits for them, and re-layouts  6.61 us

profile of v1, /device:TPU:1, one launch (start us, length us, event | category | flops | bytes accessed | tf_op | source)
XLA Modules:
  0.0 55.0 jit_solution(14200997101650877510)
XLA Ops:
  0.6 0.0 copy-start
  0.6 1.2 %copy-done = bf16[32,8,16,128]{3,2,1,0:T(8,128)(2,1)S(1)} copy-done((bf16[32,8,16,128]{3,2,1,0:T(8,128)(2,1)S(1)}, bf16[32,8,16,128]{3,2,1,0:T(8,128)(2,1)}, u32[]{:S(2)}) %copy-start) | copy-done | bytes 1048600
  1.9 0.0 copy-start.1
  1.9 1.2 %copy-done.1 = bf16[32,8,16,128]{3,2,1,0:T(8,128)(2,1)S(1)} copy-done((bf16[32,8,16,128]{3,2,1,0:T(8,128)(2,1)S(1)}, bf16[32,8,16,128]{3,2,1,0:T(8,128)(2,1)}, u32[]{:S(2)}) %copy-start.1) | copy-done | bytes 1048600
  3.1 0.0 copy-start.2
  3.1 0.8 %copy-done.2 = bf16[8,16,128]{2,1,0:T(8,128)(2,1)S(1)} copy-done((bf16[8,16,128]{2,1,0:T(8,128)(2,1)S(1)}, bf16[8,16,128]{2,1,0:T(8,128)(2,1)}, u32[]{:S(2)}) %copy-start.2) | copy-done | bytes 32792
  3.8 0.0 copy-start.3
  3.8 0.7 %copy-done.3 = s32[16,128]{1,0:T(8,128)S(1)} copy-done((s32[16,128]{1,0:T(8,128)S(1)}, s32[16,128]{1,0:T(8,128)}, u32[]{:S(2)}) %copy-start.3) | copy-done | bytes 8216
  4.5 0.0 copy-start.4
  4.5 0.7 %copy-done.4 = f32[8]{0:T(128)S(1)} copy-done((f32[8]{0:T(128)S(1)}, f32[8]{0:T(128)}, u32[]{:S(2)}) %copy-start.4) | copy-done | bytes 56
  5.2 0.0 copy-start.5
  5.2 0.7 %copy-done.5 = s32[1,4]{1,0:T(1,128)S(1)} copy-done((s32[1,4]{1,0:T(1,128)S(1)}, s32[1,4]{1,0:T(1,128)}, u32[]{:S(2)}) %copy-start.5) | copy-done | bytes 40
  5.8 47.8 %shard_map.77 = (f32[512,128]{1,0:T(8,128)S(1)}, f32[512,128]{1,0:T(8,128)S(1)}) custom-call(bf16[32,8,16,128]{3,2,1,0:T(8,128)(2,1)S(1)} %copy-done, bf16[32,8,16,128]{3,2,1,0:T(8,128)(2,1)S(1)} %copy-done.1, bf16[8,16,128]{2,1,0:T(8,128)(2,1)S(1)} %copy-done.2, f32[8]{0:T(128)S(1)} %copy-done.4, s32[16,128]{1,0:T(8,128)S(1)} %copy-done.3, s32[1,4]{1,0:T(1,128)S(1)} %copy-done.5), custom_call_target="tpu_custom_call" | custom-call | tf_op jit(solution)/shard_map/pallas_call | solution.py:432
  53.6 0.7 %copy.10 = f32[32,16,128]{2,1,0:T(8,128)} copy(f32[32,16,128]{2,1,0:T(8,128)S(1)} %bitcast.3) | data formatting | bytes 524288
  54.3 0.7 %copy.11 = f32[32,16,128]{2,1,0:T(8,128)} copy(f32[32,16,128]{2,1,0:T(8,128)S(1)} %bitcast.2) | data formatting | bytes 524288
Async XLA Ops:
  0.6 1.2 %copy-start = (bf16[32,8,16,128]{3,2,1,0:T(8,128)(2,1)S(1)}, bf16[32,8,16,128]{3,2,1,0:T(8,128)(2,1)}, u32[]{:S(2)}) copy-start(bf16[32,8,16,128]{3,2,1,0:T(8,128)(2,1)} %u_hbm.1) | copy-start | bytes 3145732
  1.9 1.2 %copy-start.1 = (bf16[32,8,16,128]{3,2,1,0:T(8,128)(2,1)S(1)}, bf16[32,8,16,128]{3,2,1,0:T(8,128)(2,1)}, u32[]{:S(2)}) copy-start(bf16[32,8,16,128]{3,2,1,0:T(8,128)(2,1)} %v_hbm.1) | copy-start | bytes 3145732
  3.1 0.8 %copy-start.2 = (bf16[8,16,128]{2,1,0:T(8,128)(2,1)S(1)}, bf16[8,16,128]{2,1,0:T(8,128)(2,1)}, u32[]{:S(2)}) copy-start(bf16[8,16,128]{2,1,0:T(8,128)(2,1)} %fraction.1) | copy-start | bytes 98308
  3.8 0.7 %copy-start.3 = (s32[16,128]{1,0:T(8,128)S(1)}, s32[16,128]{1,0:T(8,128)}, u32[]{:S(2)}) copy-start(s32[16,128]{1,0:T(8,128)} %land.1) | copy-start | bytes 24580
  4.5 0.7 %copy-start.4 = (f32[8]{0:T(128)S(1)}, f32[8]{0:T(128)}, u32[]{:S(2)}) copy-start(f32[8]{0:T(128)} %thickness.1) | copy-start | bytes 100
  5.2 0.7 %copy-start.5 = (s32[1,4]{1,0:T(1,128)S(1)}, s32[1,4]{1,0:T(1,128)}, u32[]{:S(2)}) copy-start(s32[1,4]{1,0:T(1,128)} %codes.1) | copy-start | bytes 52

commit v2 on v1

--- a/solution.py
+++ b/solution.py
@@ -83,10 +83,10 @@
 
 
 def kernel(
-    u_hbm, v_hbm, fraction, thickness, land, codes, x_out, r_out,
-    u_buf, v_buf, tu1, tv1, weight, tu2, tv2, field, g_buf, q_buf, qsum, stage,
-    edge_send, edge_recv, tu_send, tu_recv, tv_send, tv_recv, a1, b1, a2, b2,
-    load_sem, send_sem, recv_sem, ar_send, ar_recv,
+    u_hbm, v_hbm, fraction_hbm, thickness_hbm, land_hbm, codes_hbm, field, images, factors,
+    u_buf, v_buf, fraction, thickness, land, codes, tu1, tv1, weight, tu2, tv2, g_buf, q_buf, qsum, stage,
+    edge_send, edge_recv, tu_send, tu_recv, tv_send, a1, b1, a2, b2,
+    load_sem, small_sem, send_sem, recv_sem, ar_send, ar_recv,
 ):
     me = lax.axis_index("tile")
     east, west = lax.rem(me + 1, N_TILE), lax.rem(me + N_TILE - 1, N_TILE)
@@ -95,6 +95,12 @@
     plane_peers = [level * PLANE + lax.rem(place + d, PLANE) for d in range(1, PLANE)]
     level_peers = [lax.rem(level + d, DEPTH) * PLANE + place for d in range(1, DEPTH)]
 
+    small_loads = []
+    pairs = ((thickness_hbm, thickness), (codes_hbm, codes), (fraction_hbm, fraction), (land_hbm, land))
+    for n, (src, dst) in enumerate(pairs):
+        copy = pltpu.make_async_copy(src, dst, small_sem.at[n])
+        copy.start()
+        small_loads.append(copy)
     part = MEMB // CHUNKS
     loads = []
     for c in range(CHUNKS):
@@ -109,6 +115,8 @@
     for peer in greeted:
         pl.semaphore_signal(barrier, inc=1, device_id=(peer,), device_id_type=MESH)
 
+    for copy in small_loads:
+        copy.wait()
     flip = [codes[0, k] == 1 for k in range(4)]
 
     depth = None
@@ -190,23 +198,19 @@
 
     sent = []
 
-    def send_edges(k):
+    def send_rows(k):
         put_rows(k)
         copies = edges(k)
         copies[0].start()
         copies[1].start()
+        sent.extend(copies)
+        return copies
+
+    def send_columns(k, copies):
         own = put_columns(k)
         copies[2].start()
         copies[3].start()
-        sent.extend(copies)
-        return copies, own
-
-    def take_edges(k, copies, own):
-        copies[2].wait_recv()
-        copies[3].wait_recv()
-        take_columns(k, *own)
-        copies[0].wait_recv()
-        copies[1].wait_recv()
+        return own
 
     def around(k, i):
         here = inner(i)
@@ -237,18 +241,20 @@
     tv_copy.start()
     tu_copy = remote(tu_send, tu_recv, 5, 0, west)
     tu_copy.start()
-    copies, own = send_edges(0)
+    copies = send_rows(0)
+    own = send_columns(0, copies)
     tu_copy.wait_recv()
     tu2[column(32), :] = jnp.where(lanes(own_tu.shape) < 96, own_tu, tu_recv[...])
-    tv_copy.wait_recv()
-    take_edges(0, copies, own)
+    copies[2].wait_recv()
+    copies[3].wait_recv()
+    take_columns(0, *own)
 
     zero = jnp.zeros((32, 128), F32)
 
     def first(i, total):
         q = q_buf[i]
         here = inner(i)
-        below = pl.multiple_of(i * 32, 32)
+        below = i * 32 if isinstance(i, int) else pl.multiple_of(i * 32, 32)
         value = (
             tu2[here, :] - tu2[pl.ds(here.start + 1, 32), :]
             + tv2[pl.ds(below, 32), :] - tv2[pl.ds(below + 32, 32), :]
@@ -259,13 +265,18 @@
         g_buf[1, here, :] = q * value
         return total + value * value
 
-    n0 = lax.fori_loop(0, TY, first, zero, unroll=UNROLL)
-
-    def image(k, square):
-        copies, own = send_edges(k)
-        yield
-        take_edges(k, copies, own)
-
+    def middle(body, start):
+        return lax.fori_loop(1, TY - 1, body, start, unroll=UNROLL)
+
+    n0 = middle(first, zero)
+    tv_copy.wait_recv()
+    copies[0].wait_recv()
+    copies[1].wait_recv()
+    n0 = first(TY - 1, first(0, n0))
+    flight = send_rows(1)
+    own = send_columns(1, flight)
+
+    def image(k, copies, own, square):
         def step(i, totals):
             q, old = q_buf[i], field[k - 1, i]
             value = q * (qsum[i] * old - around(k, i))
@@ -277,14 +288,17 @@
             cross, own_square = totals
             return cross + old * value, own_square + value * value if square else own_square
 
-        yield lax.fori_loop(0, TY, step, (zero, zero), unroll=UNROLL)
-
-    def make_image(k, square, between=None):
-        steps = image(k, square)
-        next(steps)
-        if between is not None:
-            between()
-        return next(steps)
+        copies[2].wait_recv()
+        copies[3].wait_recv()
+        take_columns(k, *own)
+        totals = middle(step, (zero, zero))
+        copies[0].wait_recv()
+        copies[1].wait_recv()
+        totals = step(TY - 1, step(0, totals))
+        if k == 4:
+            return totals
+        ahead = send_rows(k + 1)
+        return totals, ahead, send_columns(k + 1, ahead)
 
     def fan(buf, slot, peers, phase, which):
         def copy_to(peer):
@@ -313,10 +327,12 @@
         fan_wait(buf_b, DEPTH - 1, ar_recv.at[which, 1])
         return jnp.sum(buf_b[...], axis=0)
 
-    n1, n2 = make_image(1, True)
-    n3, _ = make_image(2, False)
-    make_image(3, None, lambda: start_level(pack_sums([n0, n1, n2, n3]), a1, 0))
-    make_image(4, None, lambda: cross_levels(a1, b1, 0))
+    (n1, n2), flight, own = image(1, flight, own, True)
+    (n3, _), flight, own = image(2, flight, own, False)
+    start_level(pack_sums([n0, n1, n2, n3]), a1, 0)
+    _, flight, own = image(3, flight, own, None)
+    cross_levels(a1, b1, 0)
+    image(4, flight, own, None)
     s0, s1, s2, s3 = spread(finish(b1, 0))
 
     m0, m1, m2, m3 = s0, s0 + s1, s0 + 2.0 * s1 + s2, s0 + 3.0 * (s1 + s2) + s3
@@ -339,12 +355,9 @@
         v = [field[k, i] for k in range(5)]
         r = [c0b * v[k] + c1b * v[k + 1] + c2b * v[k + 2] for k in range(3)]
         d = [e0b * v[k] + e1b * v[k + 1] for k in range(3)]
-        here = inner(i)
         for k in range(3):
-            g_buf[k, here, :] = r[k]
-        g_buf[3, here, :] = d[0]
-        g_buf[4, here, :] = d[1]
-        tu2[here, :] = d[2]
+            images[k, i] = r[k]
+            images[3 + k, i] = d[k]
         pairs = (
             (r[0], r[0]), (r[0], d[0]), (d[0], d[0]), (r[0], r[1]),
             (r[0], d[1]), (d[0], d[1]), (r[1], r[1]), (r[1], d[1]),
@@ -397,23 +410,8 @@
     fp0, fp1, fp2 = mu - kappa, 2.0 * mu - kappa, mu
     fr0, fr1, fr2 = 1.0 + fp0 - alpha3, fp1 - alpha3, fp2
     fd0, fd1, fd2 = beta1 * fp0, beta1 * fp1, beta1 * fp2
-    cx = rows(x0, x1, xr0, xr1, xd0, xd1)
-    cr = rows(fr0, fr1, fr2, fd0, fd1, fd2)
-
-    for block in range(4):
-        xs, rs = [], []
-        for k in range(4):
-            i = 4 * block + k
-            here = inner(i)
-            r = [g_buf[n, here, :] for n in range(3)]
-            d = [g_buf[3, here, :], g_buf[4, here, :], tu2[here, :]]
-            parts = (field[0, i], field[1, i], r[0], r[1], d[0], d[1])
-            xs.append(functools.reduce(lambda s, t: s + t, [c * t for c, t in zip(cx, parts)]))
-            rs.append(functools.reduce(lambda s, t: s + t, [c * t for c, t in zip(cr, r + d)]))
-        for values, out in ((xs, x_out), (rs, r_out)):
-            t = jnp.transpose(jnp.concatenate(exchange_groups(values), axis=0))
-            for k in range(4):
-                out[pl.ds(4 * block + k, MEMB, stride=TY), :] = t[32 * k : 32 * k + 32]
+    for k, factor in enumerate((x0, x1, xr0, xr1, xd0, xd1, fr0, fr1, fr2, fd0, fd1, fd2)):
+        factors[k] = jnp.broadcast_to(factor, (8, 128))
 
     for copy in sent + [tv_copy, tu_copy]:
         copy.wait_send()
@@ -423,26 +421,59 @@
     fan_wait(b2, DEPTH - 1, ar_send.at[1, 1])
 
 
+def combine(field, images, factors, x_hbm, r_hbm, x_buf, r_buf, sem):
+    c = [jnp.concatenate([factors[k]] * 4, axis=0) for k in range(12)]
+    copies = []
+    for block in range(4):
+        xs, rs = [], []
+        for k in range(4):
+            i = 4 * block + k
+            v = [images[n, i] for n in range(6)]
+            parts = (field[0, i], field[1, i], v[0], v[1], v[3], v[4])
+            xs.append(functools.reduce(lambda s, t: s + t, [a * t for a, t in zip(c[:6], parts)]))
+            rs.append(functools.reduce(lambda s, t: s + t, [a * t for a, t in zip(c[6:], v)]))
+        for values, out in ((xs, x_buf), (rs, r_buf)):
+            t = jnp.transpose(jnp.concatenate(exchange_groups(values), axis=0))
+            for k in range(4):
+                out[pl.ds(4 * block + k, MEMB, stride=TY), :] = t[32 * k : 32 * k + 32]
+    for n, (src, dst) in enumerate(((x_buf, x_hbm), (r_buf, r_hbm))):
+        copy = pltpu.make_async_copy(src, dst, sem.at[n])
+        copy.start()
+        copies.append(copy)
+    for copy in copies:
+        copy.wait()
+
+
 def on_device(zonal, meridional, fraction, thickness, land, codes):
     vmem = pl.BlockSpec(memory_space=pltpu.VMEM)
-    smem = pl.BlockSpec(memory_space=pltpu.SMEM)
-    hbm = pl.BlockSpec(memory_space=pl.ANY)
+    hbm = pl.BlockSpec(memory_space=pltpu.HBM)
+    arguments = [
+        pltpu.with_memory_space_constraint(x, pltpu.HBM)
+        for x in (zonal, meridional, fraction, thickness, land, codes)
+    ]
     flat = jax.ShapeDtypeStruct((MEMB * TY, TX), F32)
     padded = (TY + 2) * PITCH
-    x, r = pl.pallas_call(
+    field, images, factors = pl.pallas_call(
         kernel,
-        out_shape=(flat, flat),
-        in_specs=[hbm, hbm, vmem, smem, vmem, smem],
-        out_specs=(vmem, vmem),
+        out_shape=(
+            jax.ShapeDtypeStruct((5, TY, 32, 128), F32),
+            jax.ShapeDtypeStruct((6, TY, 32, 128), F32),
+            jax.ShapeDtypeStruct((12, 8, 128), F32),
+        ),
+        in_specs=[hbm] * 6,
+        out_specs=(vmem, vmem, vmem),
         scratch_shapes=[
             pltpu.VMEM((MEMB, LEV, TY, TX), jnp.bfloat16),
             pltpu.VMEM((MEMB, LEV, TY, TX), jnp.bfloat16),
+            pltpu.VMEM((LEV, TY, TX), jnp.bfloat16),
+            pltpu.SMEM((LEV,), F32),
+            pltpu.VMEM((TY, TX), jnp.int32),
+            pltpu.SMEM((1, 4), jnp.int32),
             pltpu.VMEM((MEMB * TY, TX), F32),
             pltpu.VMEM((MEMB * TY, TX), F32),
             pltpu.VMEM((LEV, TY, TX), F32),
             pltpu.VMEM((padded, 128), F32),
             pltpu.VMEM(((TY + 1) * 32, 128), F32),
-            pltpu.VMEM((5, TY, 32, 128), F32),
             pltpu.VMEM((5, padded, 128), F32),
             pltpu.VMEM((TY, 32, 128), F32),
             pltpu.VMEM((TY, 32, 128), F32),
@@ -452,12 +483,12 @@
             pltpu.VMEM((TY, 128), F32),
             pltpu.VMEM((TY, 128), F32),
             pltpu.VMEM((32, 128), F32),
-            pltpu.VMEM((32, 128), F32),
             pltpu.VMEM((PLANE, 1, 128), F32),
             pltpu.VMEM((DEPTH, 1, 128), F32),
             pltpu.VMEM((PLANE, 4, 128), F32),
             pltpu.VMEM((DEPTH, 4, 128), F32),
             pltpu.SemaphoreType.DMA((2, CHUNKS)),
+            pltpu.SemaphoreType.DMA((4,)),
             pltpu.SemaphoreType.DMA((6, 4)),
             pltpu.SemaphoreType.DMA((6, 4)),
             pltpu.SemaphoreType.DMA((2, 2)),
@@ -466,7 +497,19 @@
         compiler_params=pltpu.CompilerParams(
             collective_id=0, has_side_effects=True, vmem_limit_bytes=40 << 20
         ),
-    )(zonal, meridional, fraction, thickness, land, codes)
+    )(*arguments)
+    x, r = pl.pallas_call(
+        combine,
+        out_shape=(flat, flat),
+        in_specs=[vmem] * 3,
+        out_specs=(hbm, hbm),
+        scratch_shapes=[
+            pltpu.VMEM((MEMB * TY, TX), F32),
+            pltpu.VMEM((MEMB * TY, TX), F32),
+            pltpu.SemaphoreType.DMA((2,)),
+        ],
+        compiler_params=pltpu.CompilerParams(vmem_limit_bytes=16 << 20),
+    )(field, images, factors)
     return x.reshape(MEMB, TY, TX), r.reshape(MEMB, TY, TX)
 
 

time: 55.3 us -> 49 us (0.89)
  local copies, waits for them, and re-layouts: 6.61 us -> 0 us
    unnamed x14 -> x0, local copies, waits for them, and re-layouts: 6.61 us -> none
    pallas_call x1 -> x2, Pallas kernels: 47.8 us -> 48.2 us  [the longest x1 46.6 us: on_device(): pl.pallas_call(kernel, out_shape=(jax.ShapeDtypeStruct((5, TY, 32, 128),...]
where the time goes in v2:
time: 49 us; the launch traced here: 48.9 us
  Pallas kernels  48.2 us (98%)
  between operations  0.64 us (1%)
    pallas_call x1, Pallas kernels, on_device(): pl.pallas_call(kernel, out_shape=(jax.ShapeDtypeStruct((5, TY, 32, 128),...  46.6 us
    pallas_call x1, Pallas kernels, on_device(): pl.pallas_call(combine, out_shape=(flat, flat), in_specs=[vmem] * 3, out_...  1.66 us

profile of v2, /device:TPU:1, one launch (start us, length us, event | category | flops | bytes accessed | tf_op | source)
XLA Modules:
  0.0 48.9 jit_solution(15346547445381365383)
XLA Ops:
  0.6 46.6 %shard_map.77 = (f32[5,16,32,128]{3,2,1,0:T(8,128)S(1)}, f32[6,16,32,128]{3,2,1,0:T(8,128)S(1)}, f32[12,8,128]{2,1,0:T(8,128)S(1)}) custom-call(bf16[32,8,16,128]{3,2,1,0:T(8,128)(2,1)} %u_hbm.1, bf16[32,8,16,128]{3,2,1,0:T(8,128)(2,1)} %v_hbm.1, bf16[8,16,128]{2,1,0:T(8,128)(2,1)} %fraction_hbm.1, f32[8]{0:T(128)} %thickness_hbm.1, s32[16,128]{1,0:T(8,128)} %land_hbm.1, ...), custom_call_target="tpu_custom_call" | custom-call | tf_op jit(solution)/shard_map/pallas_call | solution.py:456
  47.2 1.7 %shard_map.78 = (f32[512,128]{1,0:T(8,128)}, f32[512,128]{1,0:T(8,128)}) custom-call(f32[5,16,32,128]{3,2,1,0:T(8,128)S(1)} %get-tuple-element.7.field, f32[6,16,32,128]{3,2,1,0:T(8,128)S(1)} %get-tuple-element.8.images, f32[12,8,128]{2,1,0:T(8,128)S(1)} %get-tuple-element.9.factors), custom_call_target="tpu_custom_call" | custom-call | tf_op jit(solution)/shard_map/pallas_call | solution.py:501

commit v3 on v2

--- a/solution.py
+++ b/solution.py
@@ -82,15 +82,23 @@
     return out
 
 
+def pick(row, group):
+    row = jnp.where(lanes(row.shape) // 32 == group, row, 0.0)
+    row = row + roll_lanes(row, 64)
+    return row + roll_lanes(row, 32)
+
+
 def kernel(
     u_hbm, v_hbm, fraction_hbm, thickness_hbm, land_hbm, codes_hbm, field, images, factors,
     u_buf, v_buf, fraction, thickness, land, codes, tu1, tv1, weight, tu2, tv2, g_buf, q_buf, qsum, stage,
-    edge_send, edge_recv, tu_send, tu_recv, tv_send, a1, b1, a2, b2,
+    edge_send, edge_recv, tu_send, tu_recv, tv_send, tv_recv, d_recv,
+    corner_send, corner_recv, a1, b1, a2, b2,
     load_sem, small_sem, send_sem, recv_sem, ar_send, ar_recv,
 ):
     me = lax.axis_index("tile")
     east, west = lax.rem(me + 1, N_TILE), lax.rem(me + N_TILE - 1, N_TILE)
     north, south = lax.rem(me + NTX, N_TILE), lax.rem(me + N_TILE - NTX, N_TILE)
+    diagonal = {n: lax.rem(me + N_TILE + n, N_TILE) for n in (-17, -15, 15, 17)}
     level, place = me // PLANE, lax.rem(me, PLANE)
     plane_peers = [level * PLANE + lax.rem(place + d, PLANE) for d in range(1, PLANE)]
     level_peers = [lax.rem(level + d, DEPTH) * PLANE + place for d in range(1, DEPTH)]
@@ -111,7 +119,7 @@
             loads.append(copy)
 
     barrier = pltpu.get_barrier_semaphore()
-    greeted = [east, west, north, south] + plane_peers + level_peers
+    greeted = [east, west, north, south] + list(diagonal.values()) + plane_peers + level_peers
     for peer in greeted:
         pl.semaphore_signal(barrier, inc=1, device_id=(peer,), device_id_type=MESH)
 
@@ -171,20 +179,25 @@
         )
 
     def edges(k):
+        from_north, from_south = g_buf.at[k, pl.ds(17 * PITCH + 8, 32)], g_buf.at[k, pl.ds(8, 32)]
+        if k == 1:
+            from_north, from_south = d_recv.at[0], d_recv.at[1]
         return [
-            remote(edge_send.at[k, 2], g_buf.at[k, pl.ds(17 * PITCH + 8, 32)], k, 2, south),
-            remote(edge_send.at[k, 3], g_buf.at[k, pl.ds(8, 32)], k, 3, north),
+            remote(edge_send.at[k, 2], from_north, k, 2, south),
+            remote(edge_send.at[k, 3], from_south, k, 3, north),
             remote(edge_send.at[k, 0, pl.ds(0, TY)], edge_recv.at[k, 0], k, 0, west),
             remote(edge_send.at[k, 1, pl.ds(0, TY)], edge_recv.at[k, 1], k, 1, east),
         ]
 
-    def put_rows(k):
-        low, high = g_buf[k, inner(0), :], g_buf[k, inner(TY - 1), :]
+    def put_rows(k, low=None, high=None):
+        if low is None:
+            low, high = g_buf[k, inner(0), :], g_buf[k, inner(TY - 1), :]
         edge_send[k, 2] = jnp.where(flip[3], reverse_columns(low), low)
         edge_send[k, 3] = jnp.where(flip[2], reverse_columns(high), high)
 
-    def put_columns(k):
-        first, last = g_buf[k, column(0), :], g_buf[k, column(31), :]
+    def put_columns(k, first=None, last=None):
+        if first is None:
+            first, last = g_buf[k, column(0), :], g_buf[k, column(31), :]
         to_west = roll_lanes(first, 96)
         to_east = roll_lanes(last, 32)
         edge_send[k, 0, pl.ds(0, TY)] = jnp.where(flip[1], reverse_rows(to_west), to_west)
@@ -198,16 +211,16 @@
 
     sent = []
 
-    def send_rows(k):
-        put_rows(k)
+    def send_rows(k, *values):
+        put_rows(k, *values)
         copies = edges(k)
         copies[0].start()
         copies[1].start()
         sent.extend(copies)
         return copies
 
-    def send_columns(k, copies):
-        own = put_columns(k)
+    def send_columns(k, copies, *values):
+        own = put_columns(k, *values)
         copies[2].start()
         copies[3].start()
         return own
@@ -231,20 +244,55 @@
     to_groups(lambda i: tv1[pl.ds(i, MEMB, stride=TY), :], store_tv)
     to_groups(lambda i: tu1[pl.ds(i, MEMB, stride=TY), :], store_tu)
 
-    row = tv2[pl.ds(0, 32), :]
-    tv_send[...] = jnp.where(flip[3], reverse_columns(row), row)
-    own_tu = roll_lanes(tu2[column(0), :], 96)
+    tv_row = tv2[pl.ds(0, 32), :]
+    tv_send[...] = jnp.where(flip[3], reverse_columns(tv_row), tv_row)
+    tu_column = tu2[column(0), :]
+    own_tu = roll_lanes(tu_column, 96)
     tu_send[...] = jnp.where(flip[1], reverse_rows(own_tu), own_tu)
+    last_lanes = lanes(own_tu.shape) >= 96
+    tu2[column(32), :] = jnp.where(last_lanes, 0.0, own_tu)
+    tv2[pl.ds(TY * 32, 32), :] = jnp.zeros((32, 128), F32)
+
+    def part_row(i):
+        here, below = inner(i), i * 32
+        return (
+            tu2[here, :] - tu2[pl.ds(here.start + 1, 32), :]
+            + tv2[pl.ds(below, 32), :] - tv2[pl.ds(below + 32, 32), :]
+        )
+
+    def part_column(n):
+        return (
+            tu2[column(n), :] - tu2[column(n + 1), :]
+            + tv2[pl.ds(n, TY, stride=32), :] - tv2[pl.ds(n + 32, TY, stride=32), :]
+        )
+
+    low, high = tu2[pl.ds(PITCH + 8, 1), :], tu2[pl.ds(TY * PITCH + 8, 1), :]
+    left, right = pick(tv2[pl.ds(0, 1), :], 0), pick(tv2[pl.ds(31, 1), :], 3)
+    corner_send[0] = pick(jnp.where(flip[1], high, low), 0)
+    corner_send[1] = jnp.where(flip[3], right, left)
+    corner_send[2] = pick(jnp.where(flip[1], low, high), 0)
+    corner_send[3] = jnp.where(flip[3], left, right)
+
+    def corner(start, size, direction, peer):
+        at = pl.ds(start, size)
+        return remote(corner_send.at[at], corner_recv.at[at], 6, direction, peer)
 
     pl.semaphore_wait(barrier, len(greeted))
-    tv_copy = remote(tv_send, tv2.at[pl.ds(TY * 32, 32)], 5, 2, south)
+    corners = [
+        corner(0, 2, 0, diagonal[-17]), corner(2, 1, 1, diagonal[15]), corner(3, 1, 2, diagonal[-15]),
+    ]
+    for copy in corners:
+        copy.start()
+    tv_copy = remote(tv_send, tv_recv, 5, 2, south)
     tv_copy.start()
     tu_copy = remote(tu_send, tu_recv, 5, 0, west)
     tu_copy.start()
+    parts = send_rows(1, part_row(0), part_row(TY - 1))
+    send_columns(1, parts, part_column(0), part_column(31))
     copies = send_rows(0)
     own = send_columns(0, copies)
     tu_copy.wait_recv()
-    tu2[column(32), :] = jnp.where(lanes(own_tu.shape) < 96, own_tu, tu_recv[...])
+    tu2[column(32), :] = jnp.where(last_lanes, tu_recv[...], own_tu)
     copies[2].wait_recv()
     copies[3].wait_recv()
     take_columns(0, *own)
@@ -270,11 +318,35 @@
 
     n0 = middle(first, zero)
     tv_copy.wait_recv()
+    tv2[pl.ds(TY * 32, 32), :] = tv_recv[...]
     copies[0].wait_recv()
     copies[1].wait_recv()
     n0 = first(TY - 1, first(0, n0))
-    flight = send_rows(1)
-    own = send_columns(1, flight)
+    for copy in parts + corners:
+        copy.wait_recv()
+    row_shape = (32, 128)
+    position = lanes(row_shape) // 32 * 32 + lax.broadcasted_iota(jnp.int32, row_shape, 0)
+
+    def at_end(shape_position, flipped, last, value):
+        return jnp.where(shape_position == jnp.where(flipped, 0, last), value, 0.0)
+
+    north_ghost, south_ghost = pl.ds(17 * PITCH + 8, 32), pl.ds(8, 32)
+    g_buf[1, north_ghost, :] = g_buf[0, north_ghost, :] * (
+        d_recv[0] - at_end(position, flip[2], TX - 1, corner_recv[0])
+    )
+    g_buf[1, south_ghost, :] = g_buf[0, south_ghost, :] * (
+        d_recv[1] - tv_row - at_end(position, flip[3], TX - 1, corner_recv[2])
+    )
+    index = lax.broadcasted_iota(jnp.int32, (TY, 128), 0)
+    lane = lanes((TY, 128))
+    from_east = edge_recv[1, 0] - at_end(index, flip[0], TY - 1, corner_recv[1])
+    from_west = edge_recv[1, 1] - tu_column - at_end(index, flip[1], TY - 1, corner_recv[3])
+    g_buf[1, column(32), :] = jnp.where(
+        lane < 96, roll_lanes(g_buf[1, column(0), :], 96), g_buf[0, column(32), :] * from_east
+    )
+    g_buf[1, column(-1), :] = jnp.where(
+        lane >= 32, roll_lanes(g_buf[1, column(31), :], 32), g_buf[0, column(-1), :] * from_west
+    )
 
     def image(k, copies, own, square):
         def step(i, totals):
@@ -288,6 +360,11 @@
             cross, own_square = totals
             return cross + old * value, own_square + value * value if square else own_square
 
+        if k == 1:
+            totals = step(TY - 1, step(0, (zero, zero)))
+            ahead = send_rows(2)
+            totals = middle(step, totals)
+            return totals, ahead, send_columns(2, ahead)
         copies[2].wait_recv()
         copies[3].wait_recv()
         take_columns(k, *own)
@@ -327,7 +404,7 @@
         fan_wait(buf_b, DEPTH - 1, ar_recv.at[which, 1])
         return jnp.sum(buf_b[...], axis=0)
 
-    (n1, n2), flight, own = image(1, flight, own, True)
+    (n1, n2), flight, own = image(1, None, None, True)
     (n3, _), flight, own = image(2, flight, own, False)
     start_level(pack_sums([n0, n1, n2, n3]), a1, 0)
     _, flight, own = image(3, flight, own, None)
@@ -413,7 +490,7 @@
     for k, factor in enumerate((x0, x1, xr0, xr1, xd0, xd1, fr0, fr1, fr2, fd0, fd1, fd2)):
         factors[k] = jnp.broadcast_to(factor, (8, 128))
 
-    for copy in sent + [tv_copy, tu_copy]:
+    for copy in sent + corners + [tv_copy, tu_copy]:
         copy.wait_send()
     fan_wait(a1, PLANE - 1, ar_send.at[0, 0])
     fan_wait(b1, DEPTH - 1, ar_send.at[0, 1])
@@ -423,23 +500,28 @@
 
 def combine(field, images, factors, x_hbm, r_hbm, x_buf, r_buf, sem):
     c = [jnp.concatenate([factors[k]] * 4, axis=0) for k in range(12)]
+    parts = (
+        [functools.partial(lambda ref, n, i: ref[n, i], field, n) for n in (0, 1)]
+        + [functools.partial(lambda ref, n, i: ref[n, i], images, n) for n in (0, 1, 3, 4)],
+        [functools.partial(lambda ref, n, i: ref[n, i], images, n) for n in range(6)],
+    )
     copies = []
-    for block in range(4):
-        xs, rs = [], []
-        for k in range(4):
-            i = 4 * block + k
-            v = [images[n, i] for n in range(6)]
-            parts = (field[0, i], field[1, i], v[0], v[1], v[3], v[4])
-            xs.append(functools.reduce(lambda s, t: s + t, [a * t for a, t in zip(c[:6], parts)]))
-            rs.append(functools.reduce(lambda s, t: s + t, [a * t for a, t in zip(c[6:], v)]))
-        for values, out in ((xs, x_buf), (rs, r_buf)):
-            t = jnp.transpose(jnp.concatenate(exchange_groups(values), axis=0))
-            for k in range(4):
-                out[pl.ds(4 * block + k, MEMB, stride=TY), :] = t[32 * k : 32 * k + 32]
-    for n, (src, dst) in enumerate(((x_buf, x_hbm), (r_buf, r_hbm))):
-        copy = pltpu.make_async_copy(src, dst, sem.at[n])
-        copy.start()
-        copies.append(copy)
+    for half in range(2):
+        for which, (buf, hbm) in enumerate(((x_buf, x_hbm), (r_buf, r_hbm))):
+            for block in (2 * half, 2 * half + 1):
+                values = []
+                for i in range(4 * block, 4 * block + 4):
+                    terms = [f * part(i) for f, part in zip(c[6 * which : 6 * which + 6], parts[which])]
+                    values.append(functools.reduce(lambda s, t: s + t, terms))
+                t = jnp.transpose(jnp.concatenate(exchange_groups(values), axis=0))
+                for k in range(4):
+                    at = pl.ds(4 * (block % 2) + k, MEMB, stride=8)
+                    buf[half, at, :] = t[32 * k : 32 * k + 32]
+            copy = pltpu.make_async_copy(
+                buf.at[half].reshape(MEMB, 8, TX), hbm.at[:, pl.ds(8 * half, 8)], sem.at[half, which]
+            )
+            copy.start()
+            copies.append(copy)
     for copy in copies:
         copy.wait()
 
@@ -451,7 +533,7 @@
         pltpu.with_memory_space_constraint(x, pltpu.HBM)
         for x in (zonal, meridional, fraction, thickness, land, codes)
     ]
-    flat = jax.ShapeDtypeStruct((MEMB * TY, TX), F32)
+    whole = jax.ShapeDtypeStruct((MEMB, TY, TX), F32)
     padded = (TY + 2) * PITCH
     field, images, factors = pl.pallas_call(
         kernel,
@@ -483,14 +565,18 @@
             pltpu.VMEM((TY, 128), F32),
             pltpu.VMEM((TY, 128), F32),
             pltpu.VMEM((32, 128), F32),
+            pltpu.VMEM((32, 128), F32),
+            pltpu.VMEM((2, 32, 128), F32),
+            pltpu.VMEM((4, 1, 128), F32),
+            pltpu.VMEM((4, 1, 128), F32),
             pltpu.VMEM((PLANE, 1, 128), F32),
             pltpu.VMEM((DEPTH, 1, 128), F32),
             pltpu.VMEM((PLANE, 4, 128), F32),
             pltpu.VMEM((DEPTH, 4, 128), F32),
             pltpu.SemaphoreType.DMA((2, CHUNKS)),
             pltpu.SemaphoreType.DMA((4,)),
-            pltpu.SemaphoreType.DMA((6, 4)),
-            pltpu.SemaphoreType.DMA((6, 4)),
+            pltpu.SemaphoreType.DMA((7, 4)),
+            pltpu.SemaphoreType.DMA((7, 4)),
             pltpu.SemaphoreType.DMA((2, 2)),
             pltpu.SemaphoreType.DMA((2, 2)),
         ],
@@ -498,19 +584,18 @@
             collective_id=0, has_side_effects=True, vmem_limit_bytes=40 << 20
         ),
     )(*arguments)
-    x, r = pl.pallas_call(
+    return pl.pallas_call(
         combine,
-        out_shape=(flat, flat),
+        out_shape=(whole, whole),
         in_specs=[vmem] * 3,
         out_specs=(hbm, hbm),
         scratch_shapes=[
-            pltpu.VMEM((MEMB * TY, TX), F32),
-            pltpu.VMEM((MEMB * TY, TX), F32),
-            pltpu.SemaphoreType.DMA((2,)),
+            pltpu.VMEM((2, MEMB * 8, TX), F32),
+            pltpu.VMEM((2, MEMB * 8, TX), F32),
+            pltpu.SemaphoreType.DMA((2, 2)),
         ],
         compiler_params=pltpu.CompilerParams(vmem_limit_bytes=16 << 20),
     )(field, images, factors)
-    return x.reshape(MEMB, TY, TX), r.reshape(MEMB, TY, TX)
 
 
 def solution(mesh):

time: 49 us -> 44.2 us (0.902)
  Pallas kernels: 48.2 us -> 43.4 us
    pallas_call x1, Pallas kernels: 46.6 us -> 41.9 us  [on_device(): pl.pallas_call(kernel, out_shape=(jax.ShapeDtypeStruct((5, TY, 32, 128),...]
where the time goes in v3:
time: 44.2 us; the launch traced here: 44.1 us
  Pallas kernels  43.4 us (98%)
  between operations  0.64 us (1%)
    pallas_call x1, Pallas kernels, on_device(): pl.pallas_call(kernel, out_shape=(jax.ShapeDtypeStruct((5, TY, 32, 128),...  41.9 us
    pallas_call x1, Pallas kernels, on_device(): pl.pallas_call(combine, out_shape=(whole, whole), in_specs=[vmem] * 3, ou...  1.52 us

profile of v3, /device:TPU:1, one launch (start us, length us, event | category | flops | bytes accessed | tf_op | source)
XLA Modules:
  0.0 44.1 jit_solution(4797419843305929556)
XLA Ops:
  0.6 41.9 %shard_map.77 = (f32[5,16,32,128]{3,2,1,0:T(8,128)S(1)}, f32[6,16,32,128]{3,2,1,0:T(8,128)S(1)}, f32[12,8,128]{2,1,0:T(8,128)S(1)}) custom-call(bf16[32,8,16,128]{3,2,1,0:T(8,128)(2,1)} %u_hbm.1, bf16[32,8,16,128]{3,2,1,0:T(8,128)(2,1)} %v_hbm.1, bf16[8,16,128]{2,1,0:T(8,128)(2,1)} %fraction_hbm.1, f32[8]{0:T(128)} %thickness_hbm.1, s32[16,128]{1,0:T(8,128)} %land_hbm.1, ...), custom_call_target="tpu_custom_call" | custom-call | tf_op jit(solution)/shard_map/pallas_call | solution.py:538
  42.6 1.5 %shard_map.78 = (f32[32,16,128]{2,1,0:T(8,128)}, f32[32,16,128]{2,1,0:T(8,128)}) custom-call(f32[5,16,32,128]{3,2,1,0:T(8,128)S(1)} %get-tuple-element.5.field, f32[6,16,32,128]{3,2,1,0:T(8,128)S(1)} %get-tuple-element.6.images, f32[12,8,128]{2,1,0:T(8,128)S(1)} %get-tuple-element.7.factors), custom_call_target="tpu_custom_call" | custom-call | tf_op jit(solution)/shard_map/pallas_call | solution.py:587

commit v4 on v3

--- a/solution.py
+++ b/solution.py
@@ -62,7 +62,10 @@
 
 
 def pack_sums(p):
-    p = [x[0:8] + x[8:16] + (x[16:24] + x[24:32]) for x in p]
+    return fold([x[0:8] + x[8:16] + (x[16:24] + x[24:32]) for x in p])
+
+
+def fold(p):
     lane = lanes(p[0].shape)
     low = lane < 64
     even = (lane // 32) % 2 == 0
@@ -89,9 +92,9 @@
 
 
 def kernel(
-    u_hbm, v_hbm, fraction_hbm, thickness_hbm, land_hbm, codes_hbm, field, images, factors,
+    u_hbm, v_hbm, fraction_hbm, thickness_hbm, land_hbm, codes_hbm, field, factors,
     u_buf, v_buf, fraction, thickness, land, codes, tu1, tv1, weight, tu2, tv2, g_buf, q_buf, qsum, stage,
-    edge_send, edge_recv, tu_send, tu_recv, tv_send, tv_recv, d_recv,
+    edge_send, edge_recv, tu_send, tu_recv, tv_send, tv_recv, row_recv,
     corner_send, corner_recv, a1, b1, a2, b2,
     load_sem, small_sem, send_sem, recv_sem, ar_send, ar_recv,
 ):
@@ -127,6 +130,11 @@
         copy.wait()
     flip = [codes[0, k] == 1 for k in range(4)]
 
+    total = thickness[0]
+    for k in range(1, LEV):
+        total = total + thickness[k]
+    shift = 1.0 + 0.125 * total
+
     depth = None
     for k in range(LEV):
         w = thickness[k] * fraction[k].astype(F32)
@@ -179,9 +187,10 @@
         )
 
     def edges(k):
-        from_north, from_south = g_buf.at[k, pl.ds(17 * PITCH + 8, 32)], g_buf.at[k, pl.ds(8, 32)]
-        if k == 1:
-            from_north, from_south = d_recv.at[0], d_recv.at[1]
+        if k == 0:
+            from_north, from_south = g_buf.at[0, pl.ds(17 * PITCH + 8, 32)], g_buf.at[0, pl.ds(8, 32)]
+        else:
+            from_north, from_south = row_recv.at[k - 1, 0], row_recv.at[k - 1, 1]
         return [
             remote(edge_send.at[k, 2], from_north, k, 2, south),
             remote(edge_send.at[k, 3], from_south, k, 3, north),
@@ -210,6 +219,11 @@
         g_buf[k, column(-1), :] = jnp.where(lane >= 32, to_east, edge_recv[k, 1])
 
     sent = []
+    blank = jnp.zeros((32, 128), F32)
+    for k in range(2, 5):
+        if k != 3:
+            g_buf[k, pl.ds(8, 32), :] = blank
+            g_buf[k, pl.ds(17 * PITCH + 8, 32), :] = blank
 
     def send_rows(k, *values):
         put_rows(k, *values)
@@ -273,13 +287,13 @@
     corner_send[2] = pick(jnp.where(flip[1], low, high), 0)
     corner_send[3] = jnp.where(flip[3], left, right)
 
-    def corner(start, size, direction, peer):
+    def corner(start, size, index, direction, peer):
         at = pl.ds(start, size)
-        return remote(corner_send.at[at], corner_recv.at[at], 6, direction, peer)
+        return remote(corner_send.at[at], corner_recv.at[at], index, direction, peer)
 
     pl.semaphore_wait(barrier, len(greeted))
     corners = [
-        corner(0, 2, 0, diagonal[-17]), corner(2, 1, 1, diagonal[15]), corner(3, 1, 2, diagonal[-15]),
+        corner(0, 2, 6, 0, diagonal[-17]), corner(2, 1, 6, 1, diagonal[15]), corner(3, 1, 6, 2, diagonal[-15]),
     ]
     for copy in corners:
         copy.start()
@@ -308,7 +322,7 @@
             + tv2[pl.ds(below, 32), :] - tv2[pl.ds(below + 32, 32), :]
         )
         value = jnp.where(q > 0.0, value, 0.0)
-        qsum[i] = around(0, i)
+        qsum[pl.ds(below, 32), :] = q * around(0, i) + (1.0 - shift)
         field[0, i] = value
         g_buf[1, here, :] = q * value
         return total + value * value
@@ -332,10 +346,10 @@
 
     north_ghost, south_ghost = pl.ds(17 * PITCH + 8, 32), pl.ds(8, 32)
     g_buf[1, north_ghost, :] = g_buf[0, north_ghost, :] * (
-        d_recv[0] - at_end(position, flip[2], TX - 1, corner_recv[0])
+        row_recv[0, 0] - at_end(position, flip[2], TX - 1, corner_recv[0])
     )
     g_buf[1, south_ghost, :] = g_buf[0, south_ghost, :] * (
-        d_recv[1] - tv_row - at_end(position, flip[3], TX - 1, corner_recv[2])
+        row_recv[0, 1] - tv_row - at_end(position, flip[3], TX - 1, corner_recv[2])
     )
     index = lax.broadcasted_iota(jnp.int32, (TY, 128), 0)
     lane = lanes((TY, 128))
@@ -348,34 +362,46 @@
         lane >= 32, roll_lanes(g_buf[1, column(31), :], 32), g_buf[0, column(-1), :] * from_west
     )
 
-    def image(k, copies, own, square):
+    def level_of(i):
+        return pl.ds(i * 32 if isinstance(i, int) else pl.multiple_of(i * 32, 32), 32)
+
+    def step_of(k):
         def step(i, totals):
             q, old = q_buf[i], field[k - 1, i]
-            value = q * (qsum[i] * old - around(k, i))
+            value = qsum[level_of(i), :] * old - q * around(k, i)
             field[k, i] = value
             if k < 4:
                 g_buf[k + 1, inner(i), :] = q * value
-            if square is None:
-                return totals
-            cross, own_square = totals
-            return cross + old * value, own_square + value * value if square else own_square
-
-        if k == 1:
-            totals = step(TY - 1, step(0, (zero, zero)))
-            ahead = send_rows(2)
-            totals = middle(step, totals)
-            return totals, ahead, send_columns(2, ahead)
-        copies[2].wait_recv()
-        copies[3].wait_recv()
-        take_columns(k, *own)
-        totals = middle(step, (zero, zero))
-        copies[0].wait_recv()
-        copies[1].wait_recv()
-        totals = step(TY - 1, step(0, totals))
-        if k == 4:
-            return totals
-        ahead = send_rows(k + 1)
-        return totals, ahead, send_columns(k + 1, ahead)
+            return (totals[0] + old * value, totals[1] + value * value) if k == 1 else totals
+
+        return step
+
+    def flat(k):
+        return field.at[k].reshape(TY * 32, 128)
+
+    def field_column(k, n):
+        return flat(k)[pl.ds(n, TY, stride=32), :]
+
+    def inside_columns(k):
+        first_column, last_column = g_buf[k, column(0), :], g_buf[k, column(31), :]
+        g_buf[k, column(32), :] = jnp.where(lane < 96, roll_lanes(first_column, 96), 0.0)
+        g_buf[k, column(-1), :] = jnp.where(lane >= 32, roll_lanes(last_column, 32), 0.0)
+        return first_column, last_column
+
+    def add_ghosts(k, rows, columns):
+        north_row = field[k, TY - 1] - q_buf[TY - 1] * rows[0]
+        south_row = field[k, 0] - q_buf[0] * rows[1]
+        field[k, TY - 1] = north_row
+        field[k, 0] = south_row
+        east_column = field_column(k, 31) - jnp.where(lane >= 96, g_buf[0, column(31), :] * columns[0], 0.0)
+        west_column = field_column(k, 0) - jnp.where(lane < 32, g_buf[0, column(0), :] * columns[1], 0.0)
+        flat(k)[pl.ds(31, TY, stride=32), :] = east_column
+        flat(k)[pl.ds(0, TY, stride=32), :] = west_column
+        if k < 4:
+            g_buf[k + 1, inner(0), :] = q_buf[0] * south_row
+            g_buf[k + 1, inner(TY - 1), :] = q_buf[TY - 1] * north_row
+            g_buf[k + 1, column(31), :] = g_buf[0, column(31), :] * east_column
+            g_buf[k + 1, column(0), :] = g_buf[0, column(0), :] * west_column
 
     def fan(buf, slot, peers, phase, which):
         def copy_to(peer):
@@ -404,41 +430,98 @@
         fan_wait(buf_b, DEPTH - 1, ar_recv.at[which, 1])
         return jnp.sum(buf_b[...], axis=0)
 
-    (n1, n2), flight, own = image(1, None, None, True)
-    (n3, _), flight, own = image(2, flight, own, False)
-    start_level(pack_sums([n0, n1, n2, n3]), a1, 0)
-    _, flight, own = image(3, flight, own, None)
+    step = step_of(1)
+    totals = step(TY - 1, step(0, (zero, zero)))
+    flight = send_rows(2)
+    n1, n2 = middle(step, totals)
+    first_column, last_column = inside_columns(2)
+    send_columns(2, flight, first_column, last_column)
+    start, end = pl.ds(PITCH + 8, 1), pl.ds(TY * PITCH + 8, 1)
+    start_last, end_last = pl.ds(PITCH + 39, 1), pl.ds(TY * PITCH + 39, 1)
+    p00, p10 = pick(g_buf[2, start, :], 0), pick(g_buf[2, end, :], 0)
+    p01, p11 = pick(g_buf[2, start_last, :], 3), pick(g_buf[2, end_last, :], 3)
+    corner_send[4] = jnp.where(flip[1], p10, p00)
+    corner_send[5] = jnp.where(flip[3], p01, p00)
+    corner_send[6] = jnp.where(flip[0], p11, p01)
+    corner_send[7] = jnp.where(flip[3], p00, p01)
+    corner_send[8] = jnp.where(flip[1], p00, p10)
+    corner_send[9] = jnp.where(flip[2], p11, p10)
+    corner_send[10] = jnp.where(flip[0], p01, p11)
+    corner_send[11] = jnp.where(flip[2], p10, p11)
+    more_corners = [
+        corner(4 + 2 * n, 2, 7, n, diagonal[d]) for n, d in enumerate((-17, -15, 15, 17))
+    ]
+    for copy in more_corners:
+        copy.start()
+    step = step_of(2)
+    step(TY - 1, step(0, ()))
+    seconds = send_rows(3, field[2, 0], field[2, TY - 1])
+    middle(step, ())
+    send_columns(3, seconds, field_column(2, 0), field_column(2, 31))
+    start_level(pack_sums([n0, n1, n2, zero]), a1, 0)
+
+    own_rows = g_buf[2, inner(TY - 1), :], g_buf[2, inner(0), :]
+    for copy in flight:
+        copy.wait_recv()
+    add_ghosts(2, (row_recv[1, 0], row_recv[1, 1]), (edge_recv[2, 0], edge_recv[2, 1]))
+    for copy in seconds + more_corners:
+        copy.wait_recv()
+
+    def ends(shape_position, flipped, last, at_last, at_first):
+        return at_end(shape_position, flipped, last, corner_recv[at_last]) + jnp.where(
+            shape_position == jnp.where(flipped, last, 0), corner_recv[at_first], 0.0
+        )
+
+    for side, ghost, flipped, corner_slots in (
+        (0, north_ghost, flip[2], (4, 6)),
+        (1, south_ghost, flip[3], (8, 10)),
+    ):
+        q = g_buf[0, ghost, :]
+        missing = own_rows[side] + ends(position, flipped, TX - 1, *corner_slots)
+        g_buf[3, ghost, :] = q * (row_recv[2, side] - q * missing)
+    q = g_buf[0, column(32), :]
+    missing = last_column + ends(index, flip[0], TY - 1, 5, 9)
+    g_buf[3, column(32), :] = jnp.where(
+        lane < 96, roll_lanes(g_buf[3, column(0), :], 96), q * (edge_recv[3, 0] - q * missing)
+    )
+    q = g_buf[0, column(-1), :]
+    missing = first_column + ends(index, flip[1], TY - 1, 7, 11)
+    g_buf[3, column(-1), :] = jnp.where(
+        lane >= 32, roll_lanes(g_buf[3, column(31), :], 32), q * (edge_recv[3, 1] - q * missing)
+    )
+
+    step = step_of(3)
+    step(TY - 1, step(0, ()))
+    flight = send_rows(4)
+    middle(step, ())
+    send_columns(4, flight, *inside_columns(4))
     cross_levels(a1, b1, 0)
-    image(4, flight, own, None)
-    s0, s1, s2, s3 = spread(finish(b1, 0))
-
-    m0, m1, m2, m3 = s0, s0 + s1, s0 + 2.0 * s1 + s2, s0 + 3.0 * (s1 + s2) + s3
-    alpha0 = m0 / m1
-    rr1 = m0 - alpha0 * (2.0 * m1 - alpha0 * m2)
-    gain = 1.0 + rr1 / m0
-    alpha1 = rr1 / (gain * gain * m1 - alpha0 * (2.0 * gain * m2 - alpha0 * m3))
-    lead = alpha0 * alpha1
-    lin = -(alpha0 + alpha1 * gain)
-    c0, c1, c2 = 1.0 + lin + lead, lin + 2.0 * lead, lead
-    e0, e1 = gain - alpha0, -alpha0
-    x0, x1 = -lin - lead, -lead
-
-    def rows(*values):
-        return [jnp.broadcast_to(v, (32, 128)) for v in values]
-
-    c0b, c1b, c2b, e0b, e1b = rows(c0, c1, c2, e0, e1)
+    step = step_of(4)
+    middle(step, step(TY - 1, step(0, ())))
+    for copy in flight:
+        copy.wait_recv()
+    add_ghosts(4, (row_recv[3, 0], row_recv[3, 1]), (edge_recv[4, 0], edge_recv[4, 1]))
+    s0, s1, s2, _ = spread(finish(b1, 0))
+
+    c = shift
+    m1 = c * s0 + s1
+    m2 = c * (c * s0 + 2.0 * s1) + s2
+    alpha0 = s0 / m1
+    rr1 = s0 - alpha0 * (2.0 * m1 - alpha0 * m2)
+    beta0 = rr1 / s0
+    e = (1.0 - alpha0 * c, -alpha0)
+    f = (e[0] + beta0, -alpha0)
+    wide_e = [jnp.broadcast_to(x, (32, 128)) for x in e]
+    wide_f = [jnp.broadcast_to(x, (32, 128)) for x in f]
 
     def second(i, totals):
         v = [field[k, i] for k in range(5)]
-        r = [c0b * v[k] + c1b * v[k + 1] + c2b * v[k + 2] for k in range(3)]
-        d = [e0b * v[k] + e1b * v[k + 1] for k in range(3)]
-        for k in range(3):
-            images[k, i] = r[k]
-            images[3 + k, i] = d[k]
+        r = [wide_e[0] * v[k] + wide_e[1] * v[k + 1] for k in range(3)]
+        d = [wide_f[0] * v[k] + wide_f[1] * v[k + 1] for k in range(4)]
         pairs = (
-            (r[0], r[0]), (r[0], d[0]), (d[0], d[0]), (r[0], r[1]),
-            (r[0], d[1]), (d[0], d[1]), (r[1], r[1]), (r[1], d[1]),
-            (d[1], d[1]), (r[1], r[2]), (r[1], d[2]), (d[1], d[2]),
+            (r[0], r[0]), (r[0], r[1]), (r[1], r[1]), (r[1], r[2]),
+            (r[0], d[0]), (r[0], d[1]), (r[1], d[1]), (r[1], d[2]), (r[2], d[2]),
+            (d[0], d[0]), (d[0], d[1]), (d[1], d[1]), (d[1], d[2]), (d[2], d[2]), (d[2], d[3]),
         )
         out = []
         for t, (x, y) in zip(totals, pairs):
@@ -447,50 +530,64 @@
         return tuple(out)
 
     small = jnp.zeros((8, 128), F32)
-    totals = lax.fori_loop(0, TY, second, (small,) * 12, unroll=2)
-    wide = [jnp.concatenate([t, jnp.zeros((24, 128), F32)], axis=0) for t in totals]
-    packed = [pack_sums(wide[4 * k : 4 * k + 4]) for k in range(3)]
-    start_level(jnp.concatenate(packed + [packed[0] * 0.0], axis=0), a2, 1)
+    totals = lax.fori_loop(0, TY, second, (small,) * 15, unroll=2) + (small,)
+    start_level(jnp.concatenate([fold(totals[4 * k : 4 * k + 4]) for k in range(4)], axis=0), a2, 1)
     cross_levels(a2, b2, 1)
     sums = finish(b2, 1)
-    rr, rd, dd, rr_1 = spread(sums[0:1])
-    rd_1, dd_1, rr_2, rd_2 = spread(sums[1:2])
-    dd_2, rr_3, rd_3, dd_3 = spread(sums[2:3])
-    r1 = rr + rr_1
-    r2 = rr + 2.0 * rr_1 + rr_2
-    r3 = rr + 3.0 * (rr_1 + rr_2) + rr_3
-    y1 = rd + rd_1
-    y2 = rd + 2.0 * rd_1 + rd_2
-    y3 = rd + 3.0 * (rd_1 + rd_2) + rd_3
-    d1 = dd + dd_1
-    d2 = dd + 2.0 * dd_1 + dd_2
-    d3 = dd + 3.0 * (dd_1 + dd_2) + dd_3
-    beta1 = rr / rr1
-    p1 = r1 + beta1 * (2.0 * y1 + beta1 * d1)
-    p2 = r2 + beta1 * (2.0 * y2 + beta1 * d2)
-    p3 = r3 + beta1 * (2.0 * y3 + beta1 * d3)
-    rp1 = r1 + beta1 * y1
-    rp2 = r2 + beta1 * y2
-    alpha2 = rr / p1
-    rr3 = rr - alpha2 * (2.0 * rp1 - alpha2 * p2)
-    beta2 = rr3 / rr
-    q1 = (
-        r1 + alpha2 * (alpha2 * p3 - 2.0 * rp2)
-        + beta2 * (2.0 * (rp1 - alpha2 * p2) + beta2 * p1)
-    )
-    alpha3 = rr3 / q1
-    kappa = alpha2 + alpha3 * beta2
-    mu = alpha2 * alpha3
-    xp0 = kappa - mu
-    xr0, xr1 = xp0 + alpha3, -mu
-    xd0, xd1 = beta1 * xp0, -beta1 * mu
-    fp0, fp1, fp2 = mu - kappa, 2.0 * mu - kappa, mu
-    fr0, fr1, fr2 = 1.0 + fp0 - alpha3, fp1 - alpha3, fp2
-    fd0, fd1, fd2 = beta1 * fp0, beta1 * fp1, beta1 * fp2
-    for k, factor in enumerate((x0, x1, xr0, xr1, xd0, xd1, fr0, fr1, fr2, fd0, fd1, fd2)):
+    sums = [x for k in range(4) for x in spread(sums[k : k + 1])]
+    rho, sigma, delta = sums[:4], sums[4:9], sums[9:15]
+
+    def dot(a, b):
+        terms = []
+        for one, other, table in ((a[0], b[0], rho), (a[0], b[1], sigma), (a[1], b[0], sigma), (a[1], b[1], delta)):
+            for i, x in enumerate(one):
+                inner_sum = functools.reduce(lambda p, n: p + n, [y * table[i + j] for j, y in enumerate(other)], 0.0)
+                terms.append(x * inner_sum)
+        return functools.reduce(lambda p, n: p + n, terms)
+
+    def operate(a):
+        def one(p):
+            if not p:
+                return []
+            return [c * p[0]] + [p[i - 1] + c * p[i] for i in range(1, len(p))] + [p[-1]]
+
+        return one(a[0]), one(a[1])
+
+    def add(a, b, scale):
+        def one(p, n):
+            out = []
+            for i in range(max(len(p), len(n))):
+                terms = ([p[i]] if i < len(p) else []) + ([scale * n[i]] if i < len(n) else [])
+                out.append(functools.reduce(lambda x, y: x + y, terms))
+            return out
+
+        return one(a[0], b[0]), one(a[1], b[1])
+
+    unit = jnp.ones((1, 128), F32)
+    residual, direction, answer = ([unit], []), ([], [unit]), ([], [])
+    norm = rho[0]
+    for k in range(3):
+        image = operate(direction)
+        alpha = norm / dot(direction, image)
+        answer = add(answer, direction, alpha)
+        residual = add(residual, image, -alpha)
+        if k < 2:
+            after = dot(residual, residual)
+            direction = add(residual, direction, after / norm)
+            norm = after
+
+    def over_field(a, start, size):
+        out = [start] + [None] * (size - 1)
+        for values, (low_factor, high_factor) in zip(a, (e, f)):
+            for k, x in enumerate(values):
+                for n, term in ((k, x * low_factor), (k + 1, x * high_factor)):
+                    out[n] = term if out[n] is None else out[n] + term
+        return out
+
+    for k, factor in enumerate(over_field(answer, alpha0, 4) + over_field(residual, None, 5)):
         factors[k] = jnp.broadcast_to(factor, (8, 128))
 
-    for copy in sent + corners + [tv_copy, tu_copy]:
+    for copy in sent + corners + more_corners + [tv_copy, tu_copy]:
         copy.wait_send()
     fan_wait(a1, PLANE - 1, ar_send.at[0, 0])
     fan_wait(b1, DEPTH - 1, ar_send.at[0, 1])
@@ -498,20 +595,15 @@
     fan_wait(b2, DEPTH - 1, ar_send.at[1, 1])
 
 
-def combine(field, images, factors, x_hbm, r_hbm, x_buf, r_buf, sem):
-    c = [jnp.concatenate([factors[k]] * 4, axis=0) for k in range(12)]
-    parts = (
-        [functools.partial(lambda ref, n, i: ref[n, i], field, n) for n in (0, 1)]
-        + [functools.partial(lambda ref, n, i: ref[n, i], images, n) for n in (0, 1, 3, 4)],
-        [functools.partial(lambda ref, n, i: ref[n, i], images, n) for n in range(6)],
-    )
+def combine(field, factors, x_hbm, r_hbm, x_buf, r_buf, sem):
+    c = [jnp.concatenate([factors[k]] * 4, axis=0) for k in range(9)]
     copies = []
     for half in range(2):
         for which, (buf, hbm) in enumerate(((x_buf, x_hbm), (r_buf, r_hbm))):
             for block in (2 * half, 2 * half + 1):
                 values = []
                 for i in range(4 * block, 4 * block + 4):
-                    terms = [f * part(i) for f, part in zip(c[6 * which : 6 * which + 6], parts[which])]
+                    terms = [f * field[n, i] for n, f in enumerate(c[4:] if which else c[:4])]
                     values.append(functools.reduce(lambda s, t: s + t, terms))
                 t = jnp.transpose(jnp.concatenate(exchange_groups(values), axis=0))
                 for k in range(4):
@@ -535,15 +627,14 @@
     ]
     whole = jax.ShapeDtypeStruct((MEMB, TY, TX), F32)
     padded = (TY + 2) * PITCH
-    field, images, factors = pl.pallas_call(
+    field, factors = pl.pallas_call(
         kernel,
         out_shape=(
             jax.ShapeDtypeStruct((5, TY, 32, 128), F32),
-            jax.ShapeDtypeStruct((6, TY, 32, 128), F32),
-            jax.ShapeDtypeStruct((12, 8, 128), F32),
+            jax.ShapeDtypeStruct((9, 8, 128), F32),
         ),
         in_specs=[hbm] * 6,
-        out_specs=(vmem, vmem, vmem),
+        out_specs=(vmem, vmem),
         scratch_shapes=[
             pltpu.VMEM((MEMB, LEV, TY, TX), jnp.bfloat16),
             pltpu.VMEM((MEMB, LEV, TY, TX), jnp.bfloat16),
@@ -558,7 +649,7 @@
             pltpu.VMEM(((TY + 1) * 32, 128), F32),
             pltpu.VMEM((5, padded, 128), F32),
             pltpu.VMEM((TY, 32, 128), F32),
-            pltpu.VMEM((TY, 32, 128), F32),
+            pltpu.VMEM((TY * 32, 128), F32),
             pltpu.VMEM((TY, TX), F32),
             pltpu.VMEM((5, 4, 32, 128), F32),
             pltpu.VMEM((5, 2, TY, 128), F32),
@@ -566,17 +657,17 @@
             pltpu.VMEM((TY, 128), F32),
             pltpu.VMEM((32, 128), F32),
             pltpu.VMEM((32, 128), F32),
-            pltpu.VMEM((2, 32, 128), F32),
-            pltpu.VMEM((4, 1, 128), F32),
-            pltpu.VMEM((4, 1, 128), F32),
+            pltpu.VMEM((4, 2, 32, 128), F32),
+            pltpu.VMEM((12, 1, 128), F32),
+            pltpu.VMEM((12, 1, 128), F32),
             pltpu.VMEM((PLANE, 1, 128), F32),
             pltpu.VMEM((DEPTH, 1, 128), F32),
             pltpu.VMEM((PLANE, 4, 128), F32),
             pltpu.VMEM((DEPTH, 4, 128), F32),
             pltpu.SemaphoreType.DMA((2, CHUNKS)),
             pltpu.SemaphoreType.DMA((4,)),
-            pltpu.SemaphoreType.DMA((7, 4)),
-            pltpu.SemaphoreType.DMA((7, 4)),
+            pltpu.SemaphoreType.DMA((8, 4)),
+            pltpu.SemaphoreType.DMA((8, 4)),
             pltpu.SemaphoreType.DMA((2, 2)),
             pltpu.SemaphoreType.DMA((2, 2)),
         ],
@@ -587,7 +678,7 @@
     return pl.pallas_call(
         combine,
         out_shape=(whole, whole),
-        in_specs=[vmem] * 3,
+        in_specs=[vmem] * 2,
         out_specs=(hbm, hbm),
         scratch_shapes=[
             pltpu.VMEM((2, MEMB * 8, TX), F32),
@@ -595,7 +686,7 @@
             pltpu.SemaphoreType.DMA((2, 2)),
         ],
         compiler_params=pltpu.CompilerParams(vmem_limit_bytes=16 << 20),
-    )(field, images, factors)
+    )(field, factors)
 
 
 def solution(mesh):

time: 44.2 us -> 39.1 us (0.88)
  Pallas kernels: 43.4 us -> 38.4 us
    pallas_call x1, Pallas kernels: 41.9 us -> 36.9 us  [on_device(): pl.pallas_call(kernel, out_shape=(jax.ShapeDtypeStruct((5, TY, 32, 128),...]
where the time goes in v4:
time: 39.1 us; the launch traced here: 39 us
  Pallas kernels  38.4 us (98%)
  between operations  0.64 us (2%)
    pallas_call x1, Pallas kernels, on_device(): pl.pallas_call(kernel, out_shape=(jax.ShapeDtypeStruct((5, TY, 32, 128),...  36.9 us
    pallas_call x1, Pallas kernels, on_device(): pl.pallas_call(combine, out_shape=(whole, whole), in_specs=[vmem] * 2, ou...  1.52 us

profile of v4, /device:TPU:1, one launch (start us, length us, event | category | flops | bytes accessed | tf_op | source)
XLA Modules:
  0.0 39.0 jit_solution(12264762661262025360)
XLA Ops:
  0.6 36.9 %shard_map.77 = (f32[5,16,32,128]{3,2,1,0:T(8,128)S(1)}, f32[9,8,128]{2,1,0:T(8,128)S(1)}) custom-call(bf16[32,8,16,128]{3,2,1,0:T(8,128)(2,1)} %u_hbm.1, bf16[32,8,16,128]{3,2,1,0:T(8,128)(2,1)} %v_hbm.1, bf16[8,16,128]{2,1,0:T(8,128)(2,1)} %fraction_hbm.1, f32[8]{0:T(128)} %thickness_hbm.1, s32[16,128]{1,0:T(8,128)} %land_hbm.1, s32[1,4]{1,0:T(1,128)} %codes_hbm.1), custom_call_target="tpu_custom_call" | custom-call | tf_op jit(solution)/shard_map/pallas_call | solution.py:630
  37.5 1.5 %shard_map.78 = (f32[32,16,128]{2,1,0:T(8,128)}, f32[32,16,128]{2,1,0:T(8,128)}) custom-call(f32[5,16,32,128]{3,2,1,0:T(8,128)S(1)} %get-tuple-element.4.field, f32[9,8,128]{2,1,0:T(8,128)S(1)} %get-tuple-element.5.factors), custom_call_target="tpu_custom_call" | custom-call | tf_op jit(solution)/shard_map/pallas_call | solution.py:678

commit v5 on v4

--- a/solution.py
+++ b/solution.py
@@ -92,8 +92,8 @@
 
 
 def kernel(
-    u_hbm, v_hbm, fraction_hbm, thickness_hbm, land_hbm, codes_hbm, field, factors,
-    u_buf, v_buf, fraction, thickness, land, codes, tu1, tv1, weight, tu2, tv2, g_buf, q_buf, qsum, stage,
+    u_hbm, v_hbm, fraction_hbm, thickness_hbm, land_hbm, codes_hbm, turned, factors,
+    u_buf, v_buf, fraction, thickness, land, codes, tu1, tv1, weight, tu2, tv2, field, g_buf, q_buf, qsum, stage,
     edge_send, edge_recv, tu_send, tu_recv, tv_send, tv_recv, row_recv,
     corner_send, corner_recv, a1, b1, a2, b2,
     load_sem, small_sem, send_sem, recv_sem, ar_send, ar_recv,
@@ -103,8 +103,15 @@
     north, south = lax.rem(me + NTX, N_TILE), lax.rem(me + N_TILE - NTX, N_TILE)
     diagonal = {n: lax.rem(me + N_TILE + n, N_TILE) for n in (-17, -15, 15, 17)}
     level, place = me // PLANE, lax.rem(me, PLANE)
-    plane_peers = [level * PLANE + lax.rem(place + d, PLANE) for d in range(1, PLANE)]
-    level_peers = [lax.rem(level + d, DEPTH) * PLANE + place for d in range(1, DEPTH)]
+    ys = [level * PLANE + 8 * lax.rem(place // 8 + d, 4) for d in range(4)]
+    xs = [2 * lax.rem(place // 2 + d, 4) for d in range(4)]
+    cores = [lax.rem(place + d, 2) for d in range(2)]
+    offsets = sorted(
+        ((y, x, c) for y in range(4) for x in range(4) for c in range(2) if (y, x, c) != (0, 0, 0)),
+        key=lambda o: -(min(o[0], 4 - o[0]) + min(o[1], 4 - o[1])),
+    )
+    plane_peers = [ys[y] + xs[x] + cores[c] for y, x, c in offsets]
+    level_peers = [lax.rem(level + d, DEPTH) * PLANE + place for d in (4, 3, 5, 2, 6, 1, 7)]
 
     small_loads = []
     pairs = ((thickness_hbm, thickness), (codes_hbm, codes), (fraction_hbm, fraction), (land_hbm, land))
@@ -225,16 +232,17 @@
             g_buf[k, pl.ds(8, 32), :] = blank
             g_buf[k, pl.ds(17 * PITCH + 8, 32), :] = blank
 
-    def send_rows(k, *values):
-        put_rows(k, *values)
+    def send_rows(k, *values, put=True):
+        if put:
+            put_rows(k, *values)
         copies = edges(k)
         copies[0].start()
         copies[1].start()
         sent.extend(copies)
         return copies
 
-    def send_columns(k, copies, *values):
-        own = put_columns(k, *values)
+    def send_columns(k, copies, *values, put=True):
+        own = put_columns(k, *values) if put else None
         copies[2].start()
         copies[3].start()
         return own
@@ -246,6 +254,8 @@
             g_buf[k, inner(i + 1), :] + g_buf[k, inner(i - 1), :]
         )
 
+    put_rows(0)
+    own = put_columns(0)
     column_sums(u_buf, tu1, 0)
     column_sums(v_buf, tv1, 1)
 
@@ -291,6 +301,8 @@
         at = pl.ds(start, size)
         return remote(corner_send.at[at], corner_recv.at[at], index, direction, peer)
 
+    put_rows(1, part_row(0), part_row(TY - 1))
+    put_columns(1, part_column(0), part_column(31))
     pl.semaphore_wait(barrier, len(greeted))
     corners = [
         corner(0, 2, 6, 0, diagonal[-17]), corner(2, 1, 6, 1, diagonal[15]), corner(3, 1, 6, 2, diagonal[-15]),
@@ -301,10 +313,10 @@
     tv_copy.start()
     tu_copy = remote(tu_send, tu_recv, 5, 0, west)
     tu_copy.start()
-    parts = send_rows(1, part_row(0), part_row(TY - 1))
-    send_columns(1, parts, part_column(0), part_column(31))
-    copies = send_rows(0)
-    own = send_columns(0, copies)
+    parts = send_rows(1, put=False)
+    send_columns(1, parts, put=False)
+    copies = send_rows(0, put=False)
+    send_columns(0, copies, put=False)
     tu_copy.wait_recv()
     tu2[column(32), :] = jnp.where(last_lanes, tu_recv[...], own_tu)
     copies[2].wait_recv()
@@ -532,6 +544,16 @@
     small = jnp.zeros((8, 128), F32)
     totals = lax.fori_loop(0, TY, second, (small,) * 15, unroll=2) + (small,)
     start_level(jnp.concatenate([fold(totals[4 * k : 4 * k + 4]) for k in range(4)], axis=0), a2, 1)
+
+    def turn(n, carry):
+        k, block = n // 4, lax.rem(n, 4)
+        values = [field[k, 4 * block + i] for i in range(4)]
+        t = jnp.transpose(jnp.concatenate(exchange_groups(values), axis=0))
+        for i in range(4):
+            turned[k, 4 * block + i] = t[32 * i : 32 * i + 32]
+        return carry
+
+    lax.fori_loop(0, 20, turn, 0, unroll=2)
     cross_levels(a2, b2, 1)
     sums = finish(b2, 1)
     sums = [x for k in range(4) for x in spread(sums[k : k + 1])]
@@ -584,8 +606,10 @@
                     out[n] = term if out[n] is None else out[n] + term
         return out
 
-    for k, factor in enumerate(over_field(answer, alpha0, 4) + over_field(residual, None, 5)):
-        factors[k] = jnp.broadcast_to(factor, (8, 128))
+    rows = over_field(answer, alpha0, 4) + over_field(residual, None, 5)
+    columns = jnp.transpose(jnp.concatenate(rows + [jnp.zeros((119, 128), F32)], axis=0))
+    for k in range(9):
+        factors[k] = jnp.broadcast_to(columns[0:MEMB, k : k + 1], (MEMB, TX))
 
     for copy in sent + corners + more_corners + [tv_copy, tu_copy]:
         copy.wait_send()
@@ -595,20 +619,14 @@
     fan_wait(b2, DEPTH - 1, ar_send.at[1, 1])
 
 
-def combine(field, factors, x_hbm, r_hbm, x_buf, r_buf, sem):
-    c = [jnp.concatenate([factors[k]] * 4, axis=0) for k in range(9)]
+def combine(turned, factors, x_hbm, r_hbm, x_buf, r_buf, sem):
     copies = []
     for half in range(2):
         for which, (buf, hbm) in enumerate(((x_buf, x_hbm), (r_buf, r_hbm))):
-            for block in (2 * half, 2 * half + 1):
-                values = []
-                for i in range(4 * block, 4 * block + 4):
-                    terms = [f * field[n, i] for n, f in enumerate(c[4:] if which else c[:4])]
-                    values.append(functools.reduce(lambda s, t: s + t, terms))
-                t = jnp.transpose(jnp.concatenate(exchange_groups(values), axis=0))
-                for k in range(4):
-                    at = pl.ds(4 * (block % 2) + k, MEMB, stride=8)
-                    buf[half, at, :] = t[32 * k : 32 * k + 32]
+            c = [factors[k] for k in range(9)][4 * which : 4 + 5 * which]
+            for i in range(8):
+                terms = [f * turned[k, 8 * half + i] for k, f in enumerate(c)]
+                buf[half, pl.ds(i, MEMB, stride=8), :] = functools.reduce(lambda s, t: s + t, terms)
             copy = pltpu.make_async_copy(
                 buf.at[half].reshape(MEMB, 8, TX), hbm.at[:, pl.ds(8 * half, 8)], sem.at[half, which]
             )
@@ -627,11 +645,11 @@
     ]
     whole = jax.ShapeDtypeStruct((MEMB, TY, TX), F32)
     padded = (TY + 2) * PITCH
-    field, factors = pl.pallas_call(
+    turned, factors = pl.pallas_call(
         kernel,
         out_shape=(
             jax.ShapeDtypeStruct((5, TY, 32, 128), F32),
-            jax.ShapeDtypeStruct((9, 8, 128), F32),
+            jax.ShapeDtypeStruct((9, MEMB, TX), F32),
         ),
         in_specs=[hbm] * 6,
         out_specs=(vmem, vmem),
@@ -647,6 +665,7 @@
             pltpu.VMEM((LEV, TY, TX), F32),
             pltpu.VMEM((padded, 128), F32),
             pltpu.VMEM(((TY + 1) * 32, 128), F32),
+            pltpu.VMEM((5, TY, 32, 128), F32),
             pltpu.VMEM((5, padded, 128), F32),
             pltpu.VMEM((TY, 32, 128), F32),
             pltpu.VMEM((TY * 32, 128), F32),
@@ -686,7 +705,7 @@
             pltpu.SemaphoreType.DMA((2, 2)),
         ],
         compiler_params=pltpu.CompilerParams(vmem_limit_bytes=16 << 20),
-    )(field, factors)
+    )(turned, factors)
 
 
 def solution(mesh):

time: 39.1 us -> 38.4 us (0.982)
  Pallas kernels: 38.4 us -> 37.7 us
    pallas_call x1, Pallas kernels: 1.52 us -> 0.88 us  [on_device(): pl.pallas_call(combine, out_shape=(whole, whole), in_specs=[vmem] * 2, ou...]
where the time goes in v5:
time: 38.4 us; the launch traced here: 38.3 us
  Pallas kernels  37.7 us (98%)
  between operations  0.64 us (2%)
    pallas_call x1, Pallas kernels, on_device(): pl.pallas_call(kernel, out_shape=(jax.ShapeDtypeStruct((5, TY, 32, 128),...  36.8 us
    pallas_call x1, Pallas kernels, on_device(): pl.pallas_call(combine, out_shape=(whole, whole), in_specs=[vmem] * 2, ou...  0.88 us

profile of v5, /device:TPU:1, one launch (start us, length us, event | category | flops | bytes accessed | tf_op | source)
XLA Modules:
  0.0 38.3 jit_solution(12216113299826123520)
XLA Ops:
  0.6 36.8 %shard_map.77 = (f32[5,16,32,128]{3,2,1,0:T(8,128)S(1)}, f32[9,32,128]{2,1,0:T(8,128)S(1)}) custom-call(bf16[32,8,16,128]{3,2,1,0:T(8,128)(2,1)} %u_hbm.1, bf16[32,8,16,128]{3,2,1,0:T(8,128)(2,1)} %v_hbm.1, bf16[8,16,128]{2,1,0:T(8,128)(2,1)} %fraction_hbm.1, f32[8]{0:T(128)} %thickness_hbm.1, s32[16,128]{1,0:T(8,128)} %land_hbm.1, s32[1,4]{1,0:T(1,128)} %codes_hbm.1), custom_call_target="tpu_custom_call" | custom-call | tf_op jit(solution)/shard_map/pallas_call | solution.py:648
  37.4 0.9 %shard_map.78 = (f32[32,16,128]{2,1,0:T(8,128)}, f32[32,16,128]{2,1,0:T(8,128)}) custom-call(f32[5,16,32,128]{3,2,1,0:T(8,128)S(1)} %get-tuple-element.4.turned, f32[9,32,128]{2,1,0:T(8,128)S(1)} %get-tuple-element.5.factors), custom_call_target="tpu_custom_call" | custom-call | tf_op jit(solution)/shard_map/pallas_call | solution.py:697

commit v6 on v5

--- a/solution.py
+++ b/solution.py
@@ -173,18 +173,17 @@
 
     to_groups(lambda i: jnp.broadcast_to(stage[pl.ds(i, 1), :], (MEMB, TX)), store_q)
 
-    def column_sums(src, dst, n):
-        for c in range(CHUNKS):
-            loads[2 * c + n].wait()
-
-            def member(m, carry):
-                total = weight[0] * src[m, 0].astype(F32)
-                for k in range(1, LEV):
-                    total = total + weight[k] * src[m, k].astype(F32)
-                dst[pl.ds(pl.multiple_of(m * TY, TY), TY), :] = total
-                return carry
-
-            lax.fori_loop(c * part, (c + 1) * part, member, 0, unroll=2)
+    def column_sums(src, dst, n, c):
+        loads[2 * c + n].wait()
+
+        def member(m, carry):
+            total = weight[0] * src[m, 0].astype(F32)
+            for k in range(1, LEV):
+                total = total + weight[k] * src[m, k].astype(F32)
+            dst[pl.ds(pl.multiple_of(m * TY, TY), TY), :] = total
+            return carry
+
+        lax.fori_loop(c * part, (c + 1) * part, member, 0, unroll=2)
 
     def remote(src, dst, index, direction, peer):
         return pltpu.make_async_remote_copy(
@@ -256,8 +255,9 @@
 
     put_rows(0)
     own = put_columns(0)
-    column_sums(u_buf, tu1, 0)
-    column_sums(v_buf, tv1, 1)
+    for c in range(CHUNKS):
+        column_sums(u_buf, tu1, 0, c)
+        column_sums(v_buf, tv1, 1, c)
 
     def store_tu(i, value):
         tu2[inner(i), :] = value
@@ -401,12 +401,18 @@
         return first_column, last_column
 
     def add_ghosts(k, rows, columns):
-        north_row = field[k, TY - 1] - q_buf[TY - 1] * rows[0]
-        south_row = field[k, 0] - q_buf[0] * rows[1]
+        parts = (
+            q_buf[TY - 1] * rows[0],
+            q_buf[0] * rows[1],
+            jnp.where(lane >= 96, g_buf[0, column(31), :] * columns[0], 0.0),
+            jnp.where(lane < 32, g_buf[0, column(0), :] * columns[1], 0.0),
+        )
+        north_row = field[k, TY - 1] - parts[0]
+        south_row = field[k, 0] - parts[1]
         field[k, TY - 1] = north_row
         field[k, 0] = south_row
-        east_column = field_column(k, 31) - jnp.where(lane >= 96, g_buf[0, column(31), :] * columns[0], 0.0)
-        west_column = field_column(k, 0) - jnp.where(lane < 32, g_buf[0, column(0), :] * columns[1], 0.0)
+        east_column = field_column(k, 31) - parts[2]
+        west_column = field_column(k, 0) - parts[3]
         flat(k)[pl.ds(31, TY, stride=32), :] = east_column
         flat(k)[pl.ds(0, TY, stride=32), :] = west_column
         if k < 4:
@@ -414,6 +420,7 @@
             g_buf[k + 1, inner(TY - 1), :] = q_buf[TY - 1] * north_row
             g_buf[k + 1, column(31), :] = g_buf[0, column(31), :] * east_column
             g_buf[k + 1, column(0), :] = g_buf[0, column(0), :] * west_column
+        return parts
 
     def fan(buf, slot, peers, phase, which):
         def copy_to(peer):
@@ -465,12 +472,12 @@
     ]
     for copy in more_corners:
         copy.start()
+    start_level(pack_sums([n0, n1, n2, zero]), a1, 0)
     step = step_of(2)
     step(TY - 1, step(0, ()))
     seconds = send_rows(3, field[2, 0], field[2, TY - 1])
     middle(step, ())
     send_columns(3, seconds, field_column(2, 0), field_column(2, 31))
-    start_level(pack_sums([n0, n1, n2, zero]), a1, 0)
 
     own_rows = g_buf[2, inner(TY - 1), :], g_buf[2, inner(0), :]
     for copy in flight:
@@ -505,14 +512,11 @@
     step = step_of(3)
     step(TY - 1, step(0, ()))
     flight = send_rows(4)
+    cross_levels(a1, b1, 0)
     middle(step, ())
     send_columns(4, flight, *inside_columns(4))
-    cross_levels(a1, b1, 0)
     step = step_of(4)
     middle(step, step(TY - 1, step(0, ())))
-    for copy in flight:
-        copy.wait_recv()
-    add_ghosts(4, (row_recv[3, 0], row_recv[3, 1]), (edge_recv[4, 0], edge_recv[4, 1]))
     s0, s1, s2, _ = spread(finish(b1, 0))
 
     c = shift
@@ -542,7 +546,23 @@
         return tuple(out)
 
     small = jnp.zeros((8, 128), F32)
-    totals = lax.fori_loop(0, TY, second, (small,) * 15, unroll=2) + (small,)
+    totals = lax.fori_loop(0, TY, second, (small,) * 15, unroll=2)
+    for copy in flight:
+        copy.wait_recv()
+    north_part, south_part, east_part, west_part = add_ghosts(
+        4, (row_recv[3, 0], row_recv[3, 1]), (edge_recv[4, 0], edge_recv[4, 1])
+    )
+
+    def second_image(low, high):
+        n = low.shape[0]
+        return wide_f[0][0:n] * low + wide_f[1][0:n] * high
+
+    late_rows = north_part * second_image(field[2, TY - 1], field[3, TY - 1])
+    late_rows = late_rows + south_part * second_image(field[2, 0], field[3, 0])
+    late_columns = east_part * second_image(field_column(2, 31), field_column(3, 31))
+    late_columns = late_columns + west_part * second_image(field_column(2, 0), field_column(3, 0))
+    late = late_rows[0:16] + late_rows[16:32] + late_columns
+    totals = totals[:14] + (totals[14] - wide_f[1][0:8] * (late[0:8] + late[8:16]), small)
     start_level(jnp.concatenate([fold(totals[4 * k : 4 * k + 4]) for k in range(4)], axis=0), a2, 1)
 
     def turn(n, carry):

time: 38.4 us -> 38.1 us (level)
  no operation moved by 1% of the time
where the time goes in v6:
time: 38.1 us; the launch traced here: 38 us
  Pallas kernels  37.4 us (98%)
  between operations  0.64 us (2%)
    pallas_call x1, Pallas kernels, on_device(): pl.pallas_call(kernel, out_shape=(jax.ShapeDtypeStruct((5, TY, 32, 128),...  36.5 us
    pallas_call x1, Pallas kernels, on_device(): pl.pallas_call(combine, out_shape=(whole, whole), in_specs=[vmem] * 2, ou...  0.88 us

profile of v6, /device:TPU:1, one launch (start us, length us, event | category | flops | bytes accessed | tf_op | source)
XLA Modules:
  0.0 38.0 jit_solution(7465045170123504517)
XLA Ops:
  0.6 36.5 %shard_map.77 = (f32[5,16,32,128]{3,2,1,0:T(8,128)S(1)}, f32[9,32,128]{2,1,0:T(8,128)S(1)}) custom-call(bf16[32,8,16,128]{3,2,1,0:T(8,128)(2,1)} %u_hbm.1, bf16[32,8,16,128]{3,2,1,0:T(8,128)(2,1)} %v_hbm.1, bf16[8,16,128]{2,1,0:T(8,128)(2,1)} %fraction_hbm.1, f32[8]{0:T(128)} %thickness_hbm.1, s32[16,128]{1,0:T(8,128)} %land_hbm.1, s32[1,4]{1,0:T(1,128)} %codes_hbm.1), custom_call_target="tpu_custom_call" | custom-call | tf_op jit(solution)/shard_map/pallas_call | solution.py:668
  37.1 0.9 %shard_map.78 = (f32[32,16,128]{2,1,0:T(8,128)}, f32[32,16,128]{2,1,0:T(8,128)}) custom-call(f32[5,16,32,128]{3,2,1,0:T(8,128)S(1)} %get-tuple-element.4.turned, f32[9,32,128]{2,1,0:T(8,128)S(1)} %get-tuple-element.5.factors), custom_call_target="tpu_custom_call" | custom-call | tf_op jit(solution)/shard_map/pallas_call | solution.py:717

commit v7 on v6

--- a/solution.py
+++ b/solution.py
@@ -14,8 +14,8 @@
 PLANE, DEPTH = 32, 8
 N_TILE = PLANE * DEPTH
 PITCH = 48
-UNROLL = 4
-CHUNKS = 4
+UNROLL = 14
+CHUNKS = 2
 
 
 def lanes(shape):
@@ -183,7 +183,7 @@
             dst[pl.ds(pl.multiple_of(m * TY, TY), TY), :] = total
             return carry
 
-        lax.fori_loop(c * part, (c + 1) * part, member, 0, unroll=2)
+        lax.fori_loop(c * part, (c + 1) * part, member, 0, unroll=4)
 
     def remote(src, dst, index, direction, peer):
         return pltpu.make_async_remote_copy(
@@ -546,7 +546,7 @@
         return tuple(out)
 
     small = jnp.zeros((8, 128), F32)
-    totals = lax.fori_loop(0, TY, second, (small,) * 15, unroll=2)
+    totals = lax.fori_loop(0, TY, second, (small,) * 15, unroll=4)
     for copy in flight:
         copy.wait_recv()
     north_part, south_part, east_part, west_part = add_ghosts(

time: 38.1 us -> 37.8 us (level)
  Pallas kernels: 37.4 us -> 37 us
where the time goes in v7:
time: 37.8 us; the launch traced here: 37.6 us
  Pallas kernels  37 us (98%)
  between operations  0.64 us (2%)
    pallas_call x1, Pallas kernels, on_device(): pl.pallas_call(kernel, out_shape=(jax.ShapeDtypeStruct((5, TY, 32, 128),...  36.1 us
    pallas_call x1, Pallas kernels, on_device(): pl.pallas_call(combine, out_shape=(whole, whole), in_specs=[vmem] * 2, ou...  0.88 us

profile of v7, /device:TPU:1, one launch (start us, length us, event | category | flops | bytes accessed | tf_op | source)
XLA Modules:
  0.0 37.6 jit_solution(10086040743942680759)
XLA Ops:
  0.6 36.1 %shard_map.77 = (f32[5,16,32,128]{3,2,1,0:T(8,128)S(1)}, f32[9,32,128]{2,1,0:T(8,128)S(1)}) custom-call(bf16[32,8,16,128]{3,2,1,0:T(8,128)(2,1)} %u_hbm.1, bf16[32,8,16,128]{3,2,1,0:T(8,128)(2,1)} %v_hbm.1, bf16[8,16,128]{2,1,0:T(8,128)(2,1)} %fraction_hbm.1, f32[8]{0:T(128)} %thickness_hbm.1, s32[16,128]{1,0:T(8,128)} %land_hbm.1, s32[1,4]{1,0:T(1,128)} %codes_hbm.1), custom_call_target="tpu_custom_call" | custom-call | tf_op jit(solution)/shard_map/pallas_call | solution.py:668
  36.8 0.9 %shard_map.78 = (f32[32,16,128]{2,1,0:T(8,128)}, f32[32,16,128]{2,1,0:T(8,128)}) custom-call(f32[5,16,32,128]{3,2,1,0:T(8,128)S(1)} %get-tuple-element.4.turned, f32[9,32,128]{2,1,0:T(8,128)S(1)} %get-tuple-element.5.factors), custom_call_target="tpu_custom_call" | custom-call | tf_op jit(solution)/shard_map/pallas_call | solution.py:717
